TPU v7x, 128 devices: a whole 4x4x4 slice. The times are simulated.
128 devices in a mesh: seq: 16 (over y, x), dp: 8 (over z, core).
Axes of the slice: x: 4, y: 4, z: 4, core: 2. Of those that a mesh axis runs over, the one named last changes fastest.
Arguments:
- queries: bfloat16 [8, 4096, 3072], P('dp', 'seq'), may hold values from -30 to 30
- keys: bfloat16 [8, 4096, 3072], P('dp', 'seq'), may hold values from -6 to 6
- values: bfloat16 [8, 4096, 3072], P('dp', 'seq'), may hold values from -6 to 6
- grad_out: bfloat16 [8, 4096, 3072], P('dp', 'seq'), may hold values from -96 to 96
- bias_table: float32 [24, 128], P('dp'), may hold values from -4 to 4
- slot_tiles: int32 [16, 5], replicated, may hold values from 0 to 31, as said below
- live: int32 [16, 7], P('seq'), may hold values from 0 to 1, as said below
- buckets: int32 [16, 7], P('seq'), may hold values from 0 to 81
Outputs:
- query_grad: bfloat16 [8, 4096, 3072], P('dp', 'seq')
- key_grad: bfloat16 [8, 4096, 3072], P('dp', 'seq')
- value_grad: bfloat16 [8, 4096, 3072], P('dp', 'seq')
- table_grad: float32 [24, 128], P('dp')
Inputs may be any that keep to these rules, and one draw needn't show every extreme that they name: Entry s of row i names a key tile of query tile i - 1, i + 1, i - 2, i + 2 for s = 0, 1, 2, 3 and of query tile (i + 8) mod 16 for s = 4, that is, slot_tiles[i, s] // 2 is that query tile; where that query tile would lie outside 0 to 15 the entry names one of query tile i's own key tiles and is not live. `live`: entry 0 of every row is 1. Row 8 is 1 everywhere. Row 0 is 1 everywhere except entries 2 and 4.
All inputs are finite; a program needn't handle non-finite values.
Results may differ from a plain program's by a relative error of at most 0.008.
Values may be sent and summed in bfloat16 or wider, within the bound.
A program may use at most 192 MiB of HBM per device.

v0:
```python
import jax
import jax.numpy as jnp
from jax import lax
from jax.sharding import PartitionSpec as P

HEADS = 24
HEAD_DIM = 128
TOK_DEV = 256
TILE = 128
TILE_COLS = 16
SLOTS = 5
BUCKETS = 82
WIDTH = 3072
TILES_DEV = 2


NEGATIVE = -1e30
HIGHEST = lax.Precision.HIGHEST
NEAR_OFFSETS = (-1, 1, -2, 2)


def from_behind(block, axis, distance):
    devices = range(lax.axis_size(axis))
    route = [(i - distance, i) for i in devices if i - distance in devices]
    return lax.ppermute(block, axis, route)


def from_behind_2(value, axis, by):
    count = lax.axis_size(axis)
    return lax.ppermute(value, axis, [(i, (i + by) % count) for i in range(count)])


def offset_hots():
    tile_rows = TILE // TILE_COLS
    query_pos = jnp.arange(TOK_DEV, dtype=jnp.int32)[:, None]
    key_pos = jnp.arange(TILE, dtype=jnp.int32)[None, :]
    column_index = key_pos % TILE_COLS - query_pos % TILE_COLS + TILE_COLS - 1
    row_index = key_pos // TILE_COLS - query_pos // TILE_COLS % tile_rows + tile_rows - 1
    column_hot = (
        column_index.reshape(1, -1) == jnp.arange(2 * TILE_COLS - 1, dtype=jnp.int32)[:, None]
    ).astype(jnp.float32)
    row_hot = (
        row_index.reshape(1, -1) == jnp.arange(2 * tile_rows - 1, dtype=jnp.int32)[:, None]
    ).astype(jnp.float32)
    return (column_hot, row_hot)


def per_device(queries, keys, values, grad_out, bias_table, slot_tiles, live, buckets):
    axis_size = lax.axis_size("seq")
    position = lax.axis_index("seq")
    half = axis_size // 2
    scale = HEAD_DIM ** (-0.5)
    column_width = 2 * TILE_COLS - 1
    table = lax.all_gather(bias_table, "dp", axis=0, tiled=True)
    column_hot, row_hot = offset_hots()
    fine_bias = jnp.dot(table[:, BUCKETS : BUCKETS + column_width], column_hot, precision=HIGHEST)
    fine_bias = fine_bias + jnp.dot(table[:, BUCKETS + column_width :], row_hot, precision=HIGHEST)
    fine_bias = fine_bias.reshape(HEADS, TOK_DEV, TILE)
    bucket_hot = (buckets[0][:, None] == jnp.arange(BUCKETS, dtype=jnp.int32)[None, :]).astype(
        jnp.float32
    )
    coarse = jnp.dot(bucket_hot, table[:, :BUCKETS].T, precision=HIGHEST)
    alive = live[0].astype(jnp.float32)
    query_heads = queries[0].reshape(TOK_DEV, HEADS, HEAD_DIM)
    upstream_heads = grad_out[0].reshape(TOK_DEV, HEADS, HEAD_DIM)
    own_pairs = jnp.stack(
        [keys[0].reshape(TILES_DEV, TILE, WIDTH), values[0].reshape(TILES_DEV, TILE, WIDTH)], axis=1
    )

    def requested(slot, requester):
        wanted = jnp.clip(slot_tiles[requester, slot] - position * TILES_DEV, 0, TILES_DEV - 1)
        return lax.dynamic_index_in_dim(own_pairs, wanted, 0, keepdims=False)

    fetched = []
    for slot, offset in enumerate(NEAR_OFFSETS):
        requester = jnp.clip(position - offset, 0, axis_size - 1)
        fetched.append(from_behind(requested(slot, requester), "seq", -offset))
    far_requester = (position + half) % axis_size
    fetched.append(from_behind_2(requested(SLOTS - 1, far_requester), "seq", half))
    remote_pairs = jnp.stack(fetched)
    own_group = (own_pairs, coarse[:TILES_DEV], alive[:TILES_DEV])
    remote_group = (remote_pairs, coarse[TILES_DEV:], alive[TILES_DEV:])

    def scores_of(pair, coarse_row):
        key_heads = pair[0].reshape(TILE, HEADS, HEAD_DIM)
        raw = jnp.einsum("qhd,khd->hqk", query_heads, key_heads, preferred_element_type=jnp.float32)
        return raw * scale + coarse_row[:, None, None] + fine_bias

    def products_of(pair):
        value_heads = pair[1].reshape(TILE, HEADS, HEAD_DIM)
        return jnp.einsum(
            "qhd,khd->hqk", upstream_heads, value_heads, preferred_element_type=jnp.float32
        )

    def stats_step(carry, item):
        top, total, weighted = carry
        pair, coarse_row, flag = item
        scores = scores_of(pair, coarse_row)
        attend_grad = products_of(pair)
        keep = flag > 0
        new_top = jnp.where(keep, jnp.maximum(top, jnp.max(scores, axis=2, keepdims=True)), top)
        factor = jnp.exp(top - new_top)
        expo = jnp.exp(scores - new_top) * flag
        added = jnp.sum(expo, axis=2, keepdims=True)
        added_weighted = jnp.sum(expo * attend_grad, axis=2, keepdims=True)
        return ((new_top, total * factor + added, weighted * factor + added_weighted), None)

    stats = (
        jnp.full((HEADS, TOK_DEV, 1), NEGATIVE, jnp.float32),
        jnp.zeros((HEADS, TOK_DEV, 1), jnp.float32),
        jnp.zeros((HEADS, TOK_DEV, 1), jnp.float32),
    )
    stats, _ = lax.scan(stats_step, stats, own_group)
    stats, _ = lax.scan(stats_step, stats, remote_group)
    log_total = stats[0] + jnp.log(stats[1])
    delta = stats[2] / stats[1]

    def grad_step(carry, item):
        query_grad, fine_sum = carry
        pair, coarse_row, flag = item
        scores = scores_of(pair, coarse_row)
        attend = jnp.exp(scores - log_total) * flag
        attend_grad = products_of(pair)
        score_grad = attend * (attend_grad - delta)
        attend_low = attend.astype(jnp.bfloat16)
        grad_low = score_grad.astype(jnp.bfloat16)
        key_heads = pair[0].reshape(TILE, HEADS, HEAD_DIM)
        value_part = jnp.einsum(
            "hqk,qhd->khd", attend_low, upstream_heads, preferred_element_type=jnp.float32
        ).reshape(TILE, WIDTH)
        key_part = (
            jnp.einsum(
                "hqk,qhd->khd", grad_low, query_heads, preferred_element_type=jnp.float32
            ).reshape(TILE, WIDTH)
            * scale
        )
        query_grad = (
            query_grad
            + jnp.einsum("hqk,khd->qhd", grad_low, key_heads, preferred_element_type=jnp.float32)
            * scale
        )
        return (
            (query_grad, fine_sum + score_grad),
            (key_part, value_part, jnp.sum(score_grad, axis=(1, 2))),
        )

    carry = (
        jnp.zeros((TOK_DEV, HEADS, HEAD_DIM), jnp.float32),
        jnp.zeros((HEADS, TOK_DEV, TILE), jnp.float32),
    )
    carry, own_out = lax.scan(grad_step, carry, own_group)
    carry, remote_out = lax.scan(grad_step, carry, remote_group)
    query_grad, fine_sum = carry
    remote_low = jnp.stack([remote_out[0], remote_out[1]], axis=1).astype(jnp.bfloat16)

    def deposit(totals, slot, requester, arrived, weight):
        wanted = jnp.clip(slot_tiles[requester, slot] - position * TILES_DEV, 0, TILES_DEV - 1)
        pick = (jnp.arange(TILES_DEV, dtype=jnp.int32) == wanted).astype(jnp.float32)[
            :, None, None
        ] * weight
        return (
            totals[0] + pick * arrived[0].astype(jnp.float32)[None],
            totals[1] + pick * arrived[1].astype(jnp.float32)[None],
        )

    totals = (own_out[0], own_out[1])
    for slot, offset in enumerate(NEAR_OFFSETS):
        arrived = from_behind(remote_low[slot], "seq", offset)
        requester = jnp.clip(position - offset, 0, axis_size - 1)
        totals = deposit(totals, slot, requester, arrived, 1.0)
    arrived = from_behind_2(remote_low[SLOTS - 1], "seq", half)
    totals = deposit(totals, SLOTS - 1, (position + half) % axis_size, arrived, 1.0)
    block_sums = jnp.concatenate([own_out[2], remote_out[2]], axis=0)
    coarse_grad = jnp.dot(block_sums.T, bucket_hot, precision=HIGHEST)
    flat_sum = fine_sum.reshape(HEADS, TOK_DEV * TILE)
    column_grad = jnp.dot(flat_sum, column_hot.T, precision=HIGHEST)
    row_grad = jnp.dot(flat_sum, row_hot.T, precision=HIGHEST)
    table_grad = jnp.concatenate([coarse_grad, column_grad, row_grad], axis=1)
    summed = lax.psum(table_grad, "seq")
    table_out = lax.psum_scatter(summed, "dp", scatter_dimension=0, tiled=True)
    query_out = query_grad.reshape(1, TOK_DEV, WIDTH).astype(jnp.bfloat16)
    key_out = totals[0].reshape(1, TOK_DEV, WIDTH).astype(jnp.bfloat16)
    value_out = totals[1].reshape(1, TOK_DEV, WIDTH).astype(jnp.bfloat16)
    return (query_out, key_out, value_out, table_out)


def solution(mesh):
    return jax.shard_map(
        per_device,
        mesh=mesh,
        in_specs=(
            P("dp", "seq", None),
            P("dp", "seq", None),
            P("dp", "seq", None),
            P("dp", "seq", None),
            P("dp", None),
            P(),
            P("seq", None),
            P("seq", None),
        ),
        out_specs=(P("dp", "seq", None), P("dp", "seq", None), P("dp", "seq", None), P("dp", None)),
        check_vma=False,
    )
```

profile of v0, /device:TPU:0, one launch (start us, length us, event | category | flops | bytes accessed | tf_op | source)
XLA Modules:
  0.0 473.9 jit_solution(8964277425469579713)
XLA Ops:
  5.3 6.9 %fusion.41 = (bf16[2,128,3072]{2,1,0:T(8,128)(2,1)}, bf16[2,128,3072]{2,1,0:T(8,128)(2,1)}, bf16[2,128,3072]{2,1,0:T(8,128)(2,1)}, bf16[2,128,3072]{2,1,0:T(8,128)(2,1)}, bf16[2,128,3072]{2,1,0:T(8,128)(2,1)}) fusion(s32[]{:T(128)S(6)} %min.45, bf16[2,1,128,3072]{3,2,0,1:T(8,128)(2,1)} %bitcast.390, bf16[2,1,128,3072]{3,2,0,1:T(8,128)(2,1)} %bitcast.388, ...), kind=kLoop, calls=%fused_computation.108 | loop fusion | flops 3932160 | bytes 11010068 | tf_op jit(solution)/shard_map/jit(dynamic_index_in_dim)/squeeze | solution.py:72
  12.2 4.7 collective-permute-start
  18.2 6.0 %collective-permute-start.2 = (bf16[2,128,3072]{2,1,0:T(8,128)(2,1)}, bf16[2,128,3072]{2,1,0:T(8,128)(2,1)}, u32[]{:S(2)}, u32[]{:S(2)}) collective-permute-start(bf16[2,128,3072]{2,1,0:T(8,128)(2,1)} %get-tuple-element.728), channel_id=1, source_target_pairs={{0,16},{8,24},{16,32},{24,40},{32,48},{40,56},{48,64},{56,72},{64,... | collective-permute-start | bytes 4718600 | tf_op jit(solution)/shard_map/ppermute | solution.py:25
  25.5 6.3 %collective-permute-start.4 = (bf16[2,128,3072]{2,1,0:T(8,128)(2,1)}, bf16[2,128,3072]{2,1,0:T(8,128)(2,1)}, u32[]{:S(2)}, u32[]{:S(2)}) collective-permute-start(bf16[2,128,3072]{2,1,0:T(8,128)(2,1)} %get-tuple-element.725), channel_id=1, source_target_pairs={{0,64},{8,72},{16,80},{24,88},{32,96},{40,104},{48,112},{56,120},{... | collective-permute-start | bytes 4718600 | tf_op jit(solution)/shard_map/ppermute | solution.py:30
  33.7 12.8 %all-gather = f32[8,3,128]{2,1,0:T(4,128)S(1)} all-gather(f32[1,3,128]{2,1,0:T(4,128)S(1)} %bitcast.403), channel_id=1, replica_groups=mesh['seq'=16,'dp'=8] {'dp'}, dimensions={0}, use_global_device_ids=true | all-gather | bytes 13824 | tf_op jit(solution)/shard_map/all_gather | solution.py:54
  55.3 4.7 copy.171
  70.3 26.4 %while.68 = (s32[]{:T(128)}, f32[24,256,1]{1,0,2:T(8,128)S(1)}, f32[24,256,1]{1,0,2:T(8,128)S(1)}, f32[24,256,1]{1,0,2:T(8,128)S(1)}, f32[2]{0:T(128)S(1)}, /*in...) while((s32[]{:T(128)}, f32[24,256,1]{1,0,2:T(8,128)S(1)}, ...), condition=%wide.region_4.5_spmd.clone, body=%wide.region_0.4_spmd.clone.sunk | while | flops 411353088 | bytes 39764508 | solution.py:113
  104.9 15.4 %collective-permute-done.3 = bf16[2,128,3072]{2,1,0:T(8,128)(2,1)} collective-permute-done((bf16[2,128,3072]{2,1,0:T(8,128)(2,1)}, bf16[2,128,3072]{2,1,0:T(8,128)(2,1)}, u32[]{:S(2)}, u32[]{:S(2)}) %collective-permute-start.3) | collective-permute-done | bytes 1572896 | tf_op jit(solution)/shard_map/ppermute | solution.py:25
  125.6 10.6 %copy.167 = bf16[5,2,128,3072]{2,3,1,0:T(8,128)(2,1)} copy(bf16[5,2,128,3072]{3,2,1,0:T(8,128)(2,1)} %bitcast_dynamic-update-slice_fusion.4) | data formatting | bytes 15728640 | tf_op jit(solution)/shard_map/while | solution.py:114
  136.3 60.1 %while.66 = (s32[]{:T(128)}, f32[24,256,1]{1,0,2:T(8,128)S(1)}, f32[24,256,1]{1,0,2:T(8,128)S(1)}, f32[24,256,1]{1,0,2:T(8,128)S(1)}, f32[5]{0:T(128)S(1)}, /*in...) while((s32[]{:T(128)}, f32[24,256,1]{1,0,2:T(8,128)S(1)}, ...), condition=%wide.region_9.10_spmd, body=%wide.region_5.9_spmd.sunk | while | flops 411328512 | bytes 39764496 | solution.py:114
  154.6 4.5 fusion.157
  178.6 4.5 fusion.157
  196.4 46.5 %while.69 = (s32[]{:T(128)}, f32[256,24,128]{0,2,1:T(8,128)}, f32[24,256,128]{1,2,0:T(8,128)}, f32[2,128,3072]{1,2,0:T(8,128)}, f32[2,128,3072]{1,2,0:T(8,128)},...) while((s32[]{:T(128)}, f32[256,24,128]{0,2,1:T(8,128)}, ...), condition=%wide.region_12.13_spmd.clone, body=%wide.region_10.12_spmd.clone.sunk | while | flops 1018822656 | bytes 139248688 | solution.py:151
  203.2 5.4 %fusion.193 = (f32[24]{0:T(128)S(1)}, f32[24,256,128]{1,2,0:T(8,128)}, bf16[24,256,128]{1,2,0:T(8,128)(2,1)S(1)}) fusion(f32[24,256,128]{1,2,0:T(8,128)} %get-tuple-element.1210, pred[]{:T(512)S(6)} %compare.26, f32[24,256,128]{1,2,0:T(8,128)} %fusion.192, f32[24,256]{1,0:T(8,128)S(1)} %bitcast.395, bf16[128,24,128]{0,2,1:T(8,128)(2,1)} %bitcast.373, ...), kind=kOutput, calls=%fused_computation.193.clone.1 | convolution fusion | flops 206045152 | bytes 13394017 | tf_op jit(solution)/shard_map/while/body/eval_jaxpr/qhd,khd->hqk/dot_general | solution.py:91
  224.5 6.3 %fusion.193 = (f32[24]{0:T(128)S(1)}, f32[24,256,128]{1,2,0:T(8,128)}, bf16[24,256,128]{1,2,0:T(8,128)(2,1)S(1)}) fusion(f32[24,256,128]{1,2,0:T(8,128)} %get-tuple-element.1210, pred[]{:T(512)S(6)} %compare.26, f32[24,256,128]{1,2,0:T(8,128)} %fusion.192, f32[24,256]{1,0:T(8,128)S(1)} %bitcast.395, bf16[128,24,128]{0,2,1:T(8,128)(2,1)} %bitcast.373, ...), kind=kOutput, calls=%fused_computation.193.clone.1 | convolution fusion | flops 206045152 | bytes 13394017 | tf_op jit(solution)/shard_map/while/body/eval_jaxpr/qhd,khd->hqk/dot_general | solution.py:91
  237.1 5.7 %bitcast_add_fusion.17 = f32[256,24,128]{0,2,1:T(8,128)} fusion(f32[256,24,128]{0,2,1:T(8,128)} %get-tuple-element.1209, bf16[128,24,128]{0,2,1:T(8,128)(2,1)S(1)} %bitcast.368, pred[]{:T(512)S(6)} %compare.26, bf16[24,256,128]{1,2,0:T(8,128)(2,1)S(1)} %get-tuple-element.1102), kind=kOutput, calls=%fused_computation.45.clone.1 | convolution fusion | flops 203685888 | bytes 8650753 | tf_op jit(solution)/shard_map/while/body/eval_jaxpr/hqk,khd->qhd/dot_general | solution.py:139
  242.9 67.2 %while.67 = (s32[]{:T(128)}, f32[256,24,128]{0,2,1:T(8,128)}, f32[24,256,128]{1,2,0:T(8,128)}, bf16[5,128,3072]{1,2,0:T(8,128)(2,1)}, bf16[5,128,3072]{1,2,0:T(8...) while((s32[]{:T(128)}, f32[256,24,128]{0,2,1:T(8,128)}, ...), condition=%wide.region_15.16_spmd, body=%wide.region_13.15_spmd.sunk | while | flops 1017643008 | bytes 84198784 | solution.py:152
  310.1 5.9 %fusion.45 = (bf16[2,128,3072]{1,2,0:T(8,128)(2,1)}, bf16[2,128,3072]{1,2,0:T(8,128)(2,1)}, bf16[2,128,3072]{1,2,0:T(8,128)(2,1)}, bf16[2,128,3072]{1,2,0:T(8,128)(2,1)}, bf16[2,128,3072]{1,2,0:T(8,128)(2,1)}) fusion(bf16[5,1,128,3072]{2,3,0,1:T(8,128)(2,1)} %bitcast.393, bf16[5,1,128,3072]{2,3,0,1:T(8,128)(2,1)} %bitcast.394), kind=kLoop, calls=%fused_computation.112 | loop fusion | flops 3932160 | bytes 15728640 | tf_op jit(solution)/shard_map/squeeze | solution.py:168
  321.0 7.0 %collective-permute-start.6 = (bf16[2,128,3072]{1,2,0:T(8,128)(2,1)}, bf16[2,128,3072]{1,2,0:T(8,128)(2,1)}, u32[]{:S(2)}, u32[]{:S(2)}) collective-permute-start(bf16[2,128,3072]{1,2,0:T(8,128)(2,1)} %get-tuple-element.721), channel_id=1, source_target_pairs={{0,8},{8,16},{16,24},{24,32},{32,40},{40,48},{48,56},{56,64},{64,7... | collective-permute-start | bytes 4718600 | tf_op jit(solution)/shard_map/ppermute | solution.py:25
  328.0 5.6 %fusion.22 = f32[24,31]{1,0:T(8,128)S(1)} fusion(f32[3,8,256,128]{3,2,1,0:T(8,128)} %bitcast.381, s32[32768]{0:T(1024)S(1)} %copy-done.26), kind=kOutput, calls=%fused_computation.84 | convolution fusion | flops 293568512 | bytes 3279776 | tf_op jit(solution)/shard_map/dot_general | solution.py:176
  334.9 12.3 %collective-permute-start.8 = (bf16[2,128,3072]{1,2,0:T(8,128)(2,1)}, bf16[2,128,3072]{1,2,0:T(8,128)(2,1)}, u32[]{:S(2)}, u32[]{:S(2)}) collective-permute-start(bf16[2,128,3072]{1,2,0:T(8,128)(2,1)} %get-tuple-element.724), channel_id=1, source_target_pairs={{0,16},{8,24},{16,32},{24,40},{32,48},{40,56},{48,64},{56,72},{64,... | collective-permute-start | bytes 4718600 | tf_op jit(solution)/shard_map/ppermute | solution.py:25
  347.2 4.7 collective-permute-start.9
  355.8 25.6 %all-reduce = f32[24,128]{1,0:T(8,128)S(1)} all-reduce(f32[24,128]{1,0:T(8,128)S(1)} %pad_maximum_fusion.2), channel_id=2, replica_groups=mesh['seq'=16,'dp'=8] {'dp'}, use_global_device_ids=true, to_apply=%region_17.18.clone | all-reduce | flops 3072 | bytes 24576
  385.3 73.2 %psum.8 = f32[3,128]{1,0:T(4,128)} all-reduce(f32[3,128]{1,0:T(4,128)S(1)} %constant_dynamic-slice_fusion.13), channel_id=1, replica_groups=mesh['seq'=16,'dp'=8] {'seq'}, use_global_device_ids=true, to_apply=%region_16.17 | all-reduce | flops 384 | bytes 3072 | tf_op jit(solution)/shard_map/psum | solution.py:179
  (339 shorter events, 235.2 us)
Async XLA Ops:
  5.3 26.5 %copy-start.16 = (bf16[1,256,3072]{2,1,0:T(8,128)(2,1)S(1)}, bf16[1,256,3072]{2,1,0:T(8,128)(2,1)}, u32[]{:S(2)}) copy-start(bf16[1,256,3072]{2,1,0:T(8,128)(2,1)} %param.18) | copy-start | bytes 4718596
  5.3 26.5 %copy-start.17 = (bf16[1,256,3072]{2,1,0:T(8,128)(2,1)S(1)}, bf16[1,256,3072]{2,1,0:T(8,128)(2,1)}, u32[]{:S(2)}) copy-start(bf16[1,256,3072]{2,1,0:T(8,128)(2,1)} %param.17) | copy-start | bytes 4718596
  12.2 84.7 %collective-permute-start = (bf16[2,128,3072]{2,1,0:T(8,128)(2,1)}, bf16[2,128,3072]{2,1,0:T(8,128)(2,1)}, u32[]{:S(2)}, u32[]{:S(2)}) collective-permute-start(bf16[2,128,3072]{2,1,0:T(8,128)(2,1)} %get-tuple-element.726), channel_id=1, source_target_pairs={{0,8},{8,16},{16,24},{24,32},{32,40},{40,48},{48,56},{56,64},{64,7... | collective-permute-start | bytes 4718600 | tf_op jit(solution)/shard_map/ppermute | solution.py:25
  16.9 82.6 %collective-permute-start.1 = (bf16[2,128,3072]{2,1,0:T(8,128)(2,1)}, bf16[2,128,3072]{2,1,0:T(8,128)(2,1)}, u32[]{:S(2)}, u32[]{:S(2)}) collective-permute-start(bf16[2,128,3072]{2,1,0:T(8,128)(2,1)} %get-tuple-element.727), channel_id=1, source_target_pairs={{8,0},{16,8},{24,16},{32,24},{40,32},{48,40},{56,48},{64,56},{72,6... | collective-permute-start | bytes 4718600 | tf_op jit(solution)/shard_map/ppermute | solution.py:25
  18.2 84.0 %collective-permute-start.2 = (bf16[2,128,3072]{2,1,0:T(8,128)(2,1)}, bf16[2,128,3072]{2,1,0:T(8,128)(2,1)}, u32[]{:S(2)}, u32[]{:S(2)}) collective-permute-start(bf16[2,128,3072]{2,1,0:T(8,128)(2,1)} %get-tuple-element.728), channel_id=1, source_target_pairs={{0,16},{8,24},{16,32},{24,40},{32,48},{40,56},{48,64},{56,72},{64,... | collective-permute-start | bytes 4718600 | tf_op jit(solution)/shard_map/ppermute | solution.py:25
  24.2 96.1 %collective-permute-start.3 = (bf16[2,128,3072]{2,1,0:T(8,128)(2,1)}, bf16[2,128,3072]{2,1,0:T(8,128)(2,1)}, u32[]{:S(2)}, u32[]{:S(2)}) collective-permute-start(bf16[2,128,3072]{2,1,0:T(8,128)(2,1)} %get-tuple-element.729), channel_id=1, source_target_pairs={{16,0},{24,8},{32,16},{40,24},{48,32},{56,40},{64,48},{72,56},{80,... | collective-permute-start | bytes 4718600 | tf_op jit(solution)/shard_map/ppermute | solution.py:25
  25.5 97.5 %collective-permute-start.4 = (bf16[2,128,3072]{2,1,0:T(8,128)(2,1)}, bf16[2,128,3072]{2,1,0:T(8,128)(2,1)}, u32[]{:S(2)}, u32[]{:S(2)}) collective-permute-start(bf16[2,128,3072]{2,1,0:T(8,128)(2,1)} %get-tuple-element.725), channel_id=1, source_target_pairs={{0,64},{8,72},{16,80},{24,88},{32,96},{40,104},{48,112},{56,120},{... | collective-permute-start | bytes 4718600 | tf_op jit(solution)/shard_map/ppermute | solution.py:30
  65.1 5.2 %slice-start = ((f32[7,24]{1,0:T(8,128)}), f32[2,24]{1,0:T(2,128)S(1)}, s32[]{:S(2)}) async-start(f32[7,24]{1,0:T(8,128)} %copy-done.27), calls=%async_computation | async-start | bytes 2048 | tf_op jit(solution)/shard_map/slice | solution.py:81
  70.3 26.5 %copy-start.28 = (f32[7,24]{1,0:T(8,128)S(1)}, f32[7,24]{1,0:T(8,128)}, u32[]{:S(2)}) copy-start(f32[7,24]{1,0:T(8,128)} %copy-done.27) | copy-start | bytes 2020
  203.2 5.4 %copy-start.3 = (bf16[256,24,128]{0,2,1:T(8,128)(2,1)S(1)}, bf16[256,24,128]{0,2,1:T(8,128)(2,1)}, u32[]{:S(2)}) copy-start(bf16[256,24,128]{0,2,1:T(8,128)(2,1)} %get-tuple-element.1232) | copy-start | bytes 4718596 | tf_op jit(solution)/shard_map/while
  224.5 6.3 %copy-start.3 = (bf16[256,24,128]{0,2,1:T(8,128)(2,1)S(1)}, bf16[256,24,128]{0,2,1:T(8,128)(2,1)}, u32[]{:S(2)}) copy-start(bf16[256,24,128]{0,2,1:T(8,128)(2,1)} %get-tuple-element.1232) | copy-start | bytes 4718596 | tf_op jit(solution)/shard_map/while
  236.4 6.4 %copy-start.19 = (f32[2,128,3072]{1,2,0:T(8,128)}, f32[2,128,3072]{1,2,0:T(8,128)S(1)}, u32[]{:S(2)}) copy-start(f32[2,128,3072]{1,2,0:T(8,128)S(1)} %get-tuple-element.1229) | copy-start | bytes 9437188 | tf_op jit(solution)/shard_map/while
  236.4 6.4 %copy-start.22 = (f32[2,128,3072]{1,2,0:T(8,128)}, f32[2,128,3072]{1,2,0:T(8,128)S(1)}, u32[]{:S(2)}) copy-start(f32[2,128,3072]{1,2,0:T(8,128)S(1)} %get-tuple-element.1228) | copy-start | bytes 9437188 | tf_op jit(solution)/shard_map/while
  310.0 7.3 %copy-start.33 = (u32[128]{0:T(128)S(1)}, u32[128]{0:T(128)}, u32[]{:S(2)}) copy-start(u32[128]{0:T(128)} %constant.204) | copy-start | bytes 1540
  310.1 8.5 %copy-start.10 = (f32[24,256,128]{1,2,0:T(8,128)S(1)}, f32[24,256,128]{1,2,0:T(8,128)}, u32[]{:S(2)}) copy-start(f32[24,256,128]{1,2,0:T(8,128)} %get-tuple-element.279) | copy-start | bytes 9437188
  316.0 142.5 %collective-permute-start.5 = (bf16[2,128,3072]{1,2,0:T(8,128)(2,1)}, bf16[2,128,3072]{1,2,0:T(8,128)(2,1)}, u32[]{:S(2)}, u32[]{:S(2)}) collective-permute-start(bf16[2,128,3072]{1,2,0:T(8,128)(2,1)} %get-tuple-element.720), channel_id=1, source_target_pairs={{8,0},{16,8},{24,16},{32,24},{40,32},{48,40},{56,48},{64,56},{72,6... | collective-permute-start | bytes 4718600 | tf_op jit(solution)/shard_map/ppermute | solution.py:25
  318.6 9.4 %copy-start.26 = (s32[32768]{0:T(1024)S(1)}, s32[32768]{0:T(1024)}, u32[]{:S(2)}) copy-start(s32[32768]{0:T(1024)} %copy-done.25) | copy-start | bytes 393220
  321.0 30.9 %copy-start.32 = (s32[1,7]{1,0:T(1,128)S(1)}, s32[1,7]{1,0:T(1,128)}, u32[]{:S(2)}) copy-start(s32[1,7]{1,0:T(1,128)} %param.23) | copy-start | bytes 88
  321.0 31.2 %copy-start.15 = (f32[24,256,128]{2,1,0:T(8,128)S(1)}, f32[24,256,128]{2,1,0:T(8,128)}, u32[]{:S(2)}) copy-start(f32[24,256,128]{2,1,0:T(8,128)} %copy.178) | copy-start | bytes 9437188
  321.0 31.2 %copy-start.24 = (s32[32768]{0:T(1024)S(1)}, s32[32768]{0:T(1024)}, u32[]{:S(2)}) copy-start(s32[32768]{0:T(1024)} %copy-done.23) | copy-start | bytes 393220
  321.0 139.1 %collective-permute-start.6 = (bf16[2,128,3072]{1,2,0:T(8,128)(2,1)}, bf16[2,128,3072]{1,2,0:T(8,128)(2,1)}, u32[]{:S(2)}, u32[]{:S(2)}) collective-permute-start(bf16[2,128,3072]{1,2,0:T(8,128)(2,1)} %get-tuple-element.721), channel_id=1, source_target_pairs={{0,8},{8,16},{16,24},{24,32},{32,40},{40,48},{48,56},{56,64},{64,7... | collective-permute-start | bytes 4718600 | tf_op jit(solution)/shard_map/ppermute | solution.py:25
  333.6 128.1 %collective-permute-start.7 = (bf16[2,128,3072]{1,2,0:T(8,128)(2,1)}, bf16[2,128,3072]{1,2,0:T(8,128)(2,1)}, u32[]{:S(2)}, u32[]{:S(2)}) collective-permute-start(bf16[2,128,3072]{1,2,0:T(8,128)(2,1)} %get-tuple-element.722), channel_id=1, source_target_pairs={{16,0},{24,8},{32,16},{40,24},{48,32},{56,40},{64,48},{72,56},{80,... | collective-permute-start | bytes 4718600 | tf_op jit(solution)/shard_map/ppermute | solution.py:25
  334.9 128.3 %collective-permute-start.8 = (bf16[2,128,3072]{1,2,0:T(8,128)(2,1)}, bf16[2,128,3072]{1,2,0:T(8,128)(2,1)}, u32[]{:S(2)}, u32[]{:S(2)}) collective-permute-start(bf16[2,128,3072]{1,2,0:T(8,128)(2,1)} %get-tuple-element.724), channel_id=1, source_target_pairs={{0,16},{8,24},{16,32},{24,40},{32,48},{40,56},{48,64},{56,72},{64,... | collective-permute-start | bytes 4718600 | tf_op jit(solution)/shard_map/ppermute | solution.py:25
  347.2 117.6 %collective-permute-start.9 = (bf16[2,128,3072]{1,2,0:T(8,128)(2,1)}, bf16[2,128,3072]{1,2,0:T(8,128)(2,1)S(1)}, u32[]{:S(2)}, u32[]{:S(2)}) collective-permute-start(bf16[2,128,3072]{1,2,0:T(8,128)(2,1)} %get-tuple-element.723), channel_id=1, source_target_pairs={{0,64},{8,72},{16,80},{24,88},{32,96},{40,104},{48,112},{56,120},{... | collective-permute-start | bytes 4718600 | tf_op jit(solution)/shard_map/ppermute | solution.py:30
  (57 other events, 149.1 us)
where the time goes:
time: 483 us; the launch traced here: 474 us
  matrix products  133 us (28%)
  local copies, waits for them, and re-layouts  116 us (24%)
  blocking collectives  112 us (23%)
  starting transfers between devices  46.1 us (10%)
  other arithmetic  40.5 us (8%)
  waiting for transfers between devices  15.4 us (3%)
  loops' own time  5.82 us (1%)
  between operations  4.91 us (1%)
    psum x1, blocking collectives, per_device(): summed = lax.psum(table_grad, 'seq')  73.2 us
    dot_general x14, matrix products, products_of(): jnp.einsum('qhd,khd->hqk', upstream_heads, value_heads, preferred_element...  48.7 us
    ppermute x8, starting transfers between devices, from_behind(): return lax.ppermute(block, axis, route)  35.2 us
    dot_general x14, matrix products, scores_of(): jnp.einsum('qhd,khd->hqk', query_heads, key_heads, preferred_element_type...  33.7 us
    unnamed x46, local copies, waits for them, and re-layouts  32.6 us
    slice x14, local copies, waits for them, and re-layouts, products_of(): value_heads = pair[1].reshape(TILE, HEADS, HEAD_DIM)  30.5 us
    dot_general x7, matrix products, grad_step(): jnp.einsum('hqk,khd->qhd', grad_low, key_heads, preferred_element_type=jn...  29.4 us
    unnamed x1, blocking collectives  25.6 us
  transfers between devices with their start and end apart: 10, of which 1 were waited for; matrix products, arithmetic and copies ran while one was open for 18% of the time, Pallas kernels for 0%

commit v1 on v0

v1 whole, which is shorter than its diff:
```python
import jax
import jax.numpy as jnp
from jax import lax
from jax.experimental import pallas as pl
from jax.experimental.pallas import tpu as pltpu
from jax.sharding import PartitionSpec as P

HEADS = 24
HEAD_DIM = 128
TOK_DEV = 256
TILE = 128
TILE_COLS = 16
TILE_ROWS = TILE // TILE_COLS
SLOTS = 5
BUCKETS = 82
WIDTH = 3072
TILES_DEV = 2
ENTRIES = TILES_DEV + SLOTS
COLUMN_WIDTH = 2 * TILE_COLS - 1
TABLE = 128

SIDE = 4
SEQ = SIDE * SIDE
DP = 8
CHUNKS = HEADS // SIDE
NEGATIVE = -1e30
SCALE = HEAD_DIM ** (-0.5)
NEAR_OFFSETS = (-1, 1, -2, 2)
HIGHEST = lax.Precision.HIGHEST
MESH = pl.DeviceIdType.MESH

FROM_BELOW = tuple((q, s, q + o + SIDE) for q in range(SIDE) for s, o in enumerate(NEAR_OFFSETS) if q + o < 0)
FROM_ABOVE = tuple((q, s, q + o - SIDE) for q in range(SIDE) for s, o in enumerate(NEAR_OFFSETS) if q + o >= SIDE)
FROM_HALF = tuple((q, SLOTS - 1, q) for q in range(SIDE))
GROUPS = ((FROM_BELOW, 1), (FROM_ABOVE, SIDE - 1), (FROM_HALF, SIDE // 2))
LOCAL = tuple(
    (q, s, q + o) for q in range(SIDE) for s, o in enumerate(NEAR_OFFSETS) if 0 <= q + o < SIDE
)


def iota(shape, axis):
    return lax.broadcasted_iota(jnp.int32, shape, axis)


def kernel(
    queries, keys, values, upstream, table, slots, live, buckets,
    query_out, key_out, value_out, table_out,
    kv_in, qd_in, give0, give1, give2, got0, got1, got2, back0, back1, back2, home0, home1, home2,
    ret, acc, key_set, value_set, key_part, value_part,
    tables, entries, shifted, fine, fine_sum, coarse_sum, grads, grads_dp, grads_seq,
    kv_send, kv_recv, qd_send, qd_recv, give_send, got_recv, back_send, home_recv, ret_send, out_recv,
    table_send, table_recv, entry_send, entry_recv, dp_send, dp_recv, seq_send, seq_recv,
):
    gives, gots = (give0, give1, give2), (got0, got1, got2)
    backs, homes = (back0, back1, back2), (home0, home1, home2)
    outs = (query_out, key_out, value_out)
    place = lax.axis_index("seq")
    part = lax.axis_index("dp")
    x, y = lax.rem(place, SIDE), lax.div(place, SIDE)

    def seq_at(column, row):
        return {"seq": lax.rem(row, SIDE) * SIDE + lax.rem(column, SIDE)}

    def remote(source, target, send, recv, device):
        return pltpu.make_async_remote_copy(
            src_ref=source, dst_ref=target, send_sem=send, recv_sem=recv,
            device_id=device, device_id_type=MESH,
        )

    def arrived(buffer, semaphore):
        pltpu.make_async_copy(buffer, buffer, semaphore).wait()

    def head_columns(head):
        return pl.ds(pl.multiple_of(head * HEAD_DIM, HEAD_DIM), HEAD_DIM)

    barrier = pltpu.get_barrier_semaphore()
    for j in range(1, SEQ):
        pl.semaphore_signal(
            barrier, inc=1, device_id={"seq": lax.rem(place + j, SEQ)}, device_id_type=MESH
        )
    for j in range(1, DP):
        pl.semaphore_signal(
            barrier, inc=1, device_id={"dp": lax.rem(part + j, DP)}, device_id_type=MESH
        )

    lane = iota((8, TABLE), 1)
    row = iota((8, TABLE), 0)
    tables[part] = jnp.zeros((8, TABLE), jnp.float32)
    tables[part, 0 : HEADS // DP, :] = table[...]
    bucket = jnp.full((8, TABLE), -1, jnp.int32)
    alive = jnp.zeros((8, TABLE), jnp.int32)
    for e in range(ENTRIES):
        bucket = jnp.where(row == e, buckets[0, e], bucket)
        alive = jnp.where(row == e, live[0, e], alive)
    entries[x, 0] = (lane == bucket).astype(jnp.float32)
    entries[x, 1] = jnp.where(alive > 0, 0.0, NEGATIVE)
    grads[...] = jnp.zeros_like(grads)

    pl.semaphore_wait(barrier, SEQ - 1 + DP - 1)

    def table_copy(j):
        return remote(
            tables.at[part], tables.at[part], table_send.at[j], table_recv.at[part],
            {"dp": lax.rem(part + j, DP)},
        )

    def entry_copy(j):
        return remote(
            entries.at[x], entries.at[x], entry_send.at[j], entry_recv.at[x], seq_at(x + j, y)
        )

    def in_copies(refs, buffer, send, recv, c):
        copies = []
        for a, ref in enumerate(refs):
            for j in range(1, SIDE):
                to = lax.rem(x + j, SIDE)
                copies.append(
                    remote(
                        ref.at[:, head_columns(to * CHUNKS + c)], buffer.at[c, a, x],
                        send.at[c, a, j], recv.at[c], seq_at(to, y),
                    )
                )
        return copies

    def fetch(refs, buffer, send, recv, c):
        for copy in in_copies(refs, buffer, send, recv, c):
            copy.start()
        for a, ref in enumerate(refs):
            pltpu.make_async_copy(
                ref.at[:, head_columns(x * CHUNKS + c)], buffer.at[c, a, x], recv.at[c]
            ).start()

    kv = ((keys, values), kv_in, kv_send, kv_recv)
    qd = ((queries, upstream), qd_in, qd_send, qd_recv)

    def give_copy(g, c):
        return remote(
            gives[g].at[c], gots[g].at[c], give_send.at[c, g], got_recv.at[c, g],
            seq_at(x, y + GROUPS[g][1]),
        )

    def back_copy(g, c):
        return remote(
            backs[g].at[c], homes[g].at[c], back_send.at[c, g], home_recv.at[c, g],
            seq_at(x, y + SIDE - GROUPS[g][1]),
        )

    def ret_copies(a, c):
        return [
            remote(
                ret.at[c, a, lax.rem(x + j, SIDE)], outs[a].at[:, head_columns(x * CHUNKS + c)],
                ret_send.at[c, a, j], out_recv.at[a], seq_at(x + j, y),
            )
            for j in range(1, SIDE)
        ]

    def give_back(a, c):
        for copy in ret_copies(a, c):
            copy.start()
        pltpu.make_async_copy(
            ret.at[c, a, x], outs[a].at[:, head_columns(x * CHUNKS + c)], out_recv.at[a]
        ).start()

    def upper(query_row, q, s):
        return lax.rem(slots[lax.rem(query_row, SIDE) * SIDE + q, s], TILES_DEV) == 1

    for j in range(1, DP):
        table_copy(j).start()
    for j in range(1, SIDE):
        entry_copy(j).start()
    fetch(*kv, 0)
    fetch(*qd, 0)
    fetch(*kv, 1)
    for j in range(1, DP):
        source = lax.rem(part + j, DP)
        arrived(tables.at[source], table_recv.at[source])
    for j in range(1, SIDE):
        source = lax.rem(x + j, SIDE)
        arrived(entries.at[source], entry_recv.at[source])

    def halves(c, a, tile):
        return kv_in[c, a, tile, 0:TILE, :], kv_in[c, a, tile, TILE : 2 * TILE, :]

    def send_tiles(c):
        arrived(kv_in.at[c], kv_recv.at[c])

        @pl.when(c + 1 < CHUNKS)
        def _():
            fetch(*qd, c + 1)

        @pl.when(c + 2 < CHUNKS)
        def _():
            fetch(*kv, c + 2)

        for g, (group, distance) in enumerate(GROUPS):
            for n, (q, s, tile) in enumerate(group):
                pick = upper(y + distance, q, s)
                for a in range(2):
                    low, high = halves(c, a, tile)
                    gives[g][c, a, n] = jnp.where(pick, high, low)
            give_copy(g, c).start()

    def compute(c):
        arrived(qd_in.at[c], qd_recv.at[c])
        for g in range(3):
            arrived(gots[g].at[c], got_recv.at[c, g])
        sets = (key_set, value_set)
        for a in range(2):
            for q in range(SIDE):
                sets[a][q, 0 : 2 * TILE, :] = kv_in[c, a, q]
            for q, s, tile in LOCAL:
                low, high = halves(c, a, tile)
                at = (TILES_DEV + s) * TILE
                sets[a][q, at : at + TILE, :] = jnp.where(upper(y, q, s), high, low)
            for g, (group, _) in enumerate(GROUPS):
                for n, (q, s, _) in enumerate(group):
                    at = (TILES_DEV + s) * TILE
                    sets[a][q, at : at + TILE, :] = gots[g][c, a, n]

        head_row = tables[2 * x + lax.div(c, 3), pl.ds(lax.rem(c, 3), 1), :]
        for j in range(TILE_COLS):
            shifted[j : j + 1, :] = pltpu.roll(head_row, (2 * TABLE - BUCKETS - j) % TABLE, 1)
        for j in range(TILE_ROWS):
            shifted[TILE_COLS + j : TILE_COLS + j + 1, :] = pltpu.roll(
                head_row, (2 * TABLE - BUCKETS - COLUMN_WIDTH - j) % TABLE, 1
            )
        offset = iota((TABLE, TILE), 0)
        query_at = iota((TABLE, TILE), 1)
        column_hot = (offset == TILE_COLS - 1 - lax.rem(query_at, TILE_COLS)).astype(jnp.float32)
        row_hot = (offset == TILE_ROWS - 1 - lax.div(query_at, TILE_COLS)).astype(jnp.float32)
        column_bias = jnp.dot(
            shifted[0:TILE_COLS, :], column_hot, precision=HIGHEST,
            preferred_element_type=jnp.float32,
        )
        row_bias = jnp.dot(
            shifted[TILE_COLS : TILE_COLS + TILE_ROWS, :], row_hot, precision=HIGHEST,
            preferred_element_type=jnp.float32,
        )
        for j in range(TILE_ROWS):
            band = column_bias + row_bias[j : j + 1, :]
            fine[j * TILE_COLS : (j + 1) * TILE_COLS, 0:TILE] = band
            fine[j * TILE_COLS : (j + 1) * TILE_COLS, TILE : 2 * TILE] = band
        fine_sum[...] = jnp.zeros_like(fine_sum)
        coarse_sum[...] = jnp.zeros_like(coarse_sum)

        def one_query_tile(q, carry):
            query = qd_in[c, 0, q]
            grad = qd_in[c, 1, q]
            key = key_set[q]
            value = value_set[q]
            hot = entries[q, 0]
            entry_bias = jnp.sum(hot * head_row, axis=1, keepdims=True) + entries[q, 1][:, 0:1]
            both = (((1,), (1,)), ((), ()))
            raw = lax.dot_general(key, query, both, preferred_element_type=jnp.float32)
            product = lax.dot_general(value, grad, both, preferred_element_type=jnp.float32)
            fine_bias = fine[...]
            scores = [
                raw[e * TILE : (e + 1) * TILE, :] * SCALE + (fine_bias + entry_bias[e : e + 1, :])
                for e in range(ENTRIES)
            ]
            attend_grad = [product[e * TILE : (e + 1) * TILE, :] for e in range(ENTRIES)]
            top = scores[0]
            for e in range(1, ENTRIES):
                top = jnp.maximum(top, scores[e])
            top = jnp.max(top, axis=0, keepdims=True)
            expo = [jnp.exp(block - top) for block in scores]
            total, weighted = expo[0], expo[0] * attend_grad[0]
            for e in range(1, ENTRIES):
                total = total + expo[e]
                weighted = weighted + expo[e] * attend_grad[e]
            inverse = 1.0 / jnp.sum(total, axis=0, keepdims=True)
            delta = jnp.sum(weighted, axis=0, keepdims=True) * inverse
            attend = [block * inverse for block in expo]
            score_grad = [attend[e] * (attend_grad[e] - delta) for e in range(ENTRIES)]
            attend_low = jnp.concatenate([b.astype(jnp.bfloat16) for b in attend], axis=0)
            grad_low = jnp.concatenate([b.astype(jnp.bfloat16) for b in score_grad], axis=0)
            value_part[q] = jnp.dot(attend_low, grad, preferred_element_type=jnp.float32)
            key_part[q] = jnp.dot(grad_low, query, preferred_element_type=jnp.float32) * SCALE
            query_grad = lax.dot_general(
                key, grad_low, (((0,), (0,)), ((), ())), preferred_element_type=jnp.float32
            )
            ret[c, 0, q] = (query_grad.T * SCALE).astype(jnp.bfloat16)
            total_grad = score_grad[0]
            for e in range(1, ENTRIES):
                total_grad = total_grad + score_grad[e]
            fine_sum[...] += total_grad[:, 0:TILE] + total_grad[:, TILE : 2 * TILE]
            coarse = jnp.zeros((1, TABLE), jnp.float32)
            for e in range(ENTRIES):
                block_sum = jnp.sum(score_grad[e], axis=0, keepdims=True)
                coarse = coarse + jnp.sum(block_sum, axis=1, keepdims=True) * hot[e : e + 1, :]
            coarse_sum[0:1, :] += coarse
            return carry

        lax.fori_loop(0, SIDE, one_query_tile, 0)
        give_back(0, c)
        parts = (key_part, value_part)
        for g, (group, _) in enumerate(GROUPS):
            for n, (q, s, _) in enumerate(group):
                at = (TILES_DEV + s) * TILE
                for a in range(2):
                    backs[g][c, a, n] = parts[a][q, at : at + TILE, :].astype(jnp.bfloat16)
            back_copy(g, c).start()
        slot = lax.rem(c, 2)
        for a in range(2):
            for q in range(SIDE):
                acc[slot, a, q] = parts[a][q, 0 : 2 * TILE, :]
            for q, s, tile in LOCAL:
                at = (TILES_DEV + s) * TILE
                deposit(slot, a, tile, upper(y, q, s), parts[a][q, at : at + TILE, :])

        folded = fine_sum[...].reshape(TILE_ROWS, TILE_COLS, TILE)
        across = (((1,), (1,)), ((), ()))
        column_grad = lax.dot_general(
            jnp.sum(folded, axis=0), column_hot, across, precision=HIGHEST,
            preferred_element_type=jnp.float32,
        )
        row_grad = lax.dot_general(
            jnp.sum(folded, axis=1), row_hot, across, precision=HIGHEST,
            preferred_element_type=jnp.float32,
        )
        table_row = coarse_sum[0:1, :]
        for j in range(TILE_COLS):
            table_row = table_row + pltpu.roll(column_grad[j : j + 1, :], BUCKETS + j, 1)
        for j in range(TILE_ROWS):
            table_row = table_row + pltpu.roll(
                row_grad[j : j + 1, :], BUCKETS + COLUMN_WIDTH + j, 1
            )
        grads[pl.ds(c, 1), :] = table_row

    def deposit(slot, a, tile, pick, partial):
        acc[slot, a, tile, 0:TILE, :] += jnp.where(pick, 0.0, partial)
        acc[slot, a, tile, TILE : 2 * TILE, :] += jnp.where(pick, partial, 0.0)

    def finish(c):
        slot = lax.rem(c, 2)
        for g, (group, distance) in enumerate(GROUPS):
            arrived(homes[g].at[c], home_recv.at[c, g])
            for n, (q, s, tile) in enumerate(group):
                pick = upper(y + distance, q, s)
                for a in range(2):
                    deposit(slot, a, tile, pick, homes[g][c, a, n].astype(jnp.float32))
        for a in range(2):
            for q in range(SIDE):
                ret[c, 1 + a, q] = acc[slot, a, q].astype(jnp.bfloat16)
            give_back(1 + a, c)

    def dp_copy(j):
        return remote(
            grads, grads_dp.at[part], dp_send.at[j], dp_recv.at[part],
            {"dp": lax.rem(part + j, DP)},
        )

    def seq_copy(j):
        return remote(
            grads_seq.at[place], grads_seq.at[place], seq_send.at[j], seq_recv.at[place],
            {"seq": lax.rem(place + j, SEQ)},
        )

    def step(t, carry):
        @pl.when(t < CHUNKS)
        def _():
            send_tiles(t)

        @pl.when((t >= 1) & (t < CHUNKS + 1))
        def _():
            compute(t - 1)

        @pl.when(t >= 2)
        def _():
            finish(t - 2)

        return carry

    lax.fori_loop(0, CHUNKS + 1, step, 0)

    for j in range(1, DP):
        dp_copy(j).start()
    total = grads[...]
    for j in range(1, DP):
        source = lax.rem(part + j, DP)
        arrived(grads_dp.at[source], dp_recv.at[source])
        total = total + grads_dp[source]
    grads_seq[place] = total
    for j in range(1, SEQ):
        seq_copy(j).start()
    finish(CHUNKS - 1)
    for j in range(1, SEQ):
        source = lax.rem(place + j, SEQ)
        arrived(grads_seq.at[source], seq_recv.at[source])
    owner = lax.div(part, 2)
    mine = grads_seq[owner]
    for j in range(1, SIDE):
        mine = mine + grads_seq[owner + j * SIDE]
    own = HEADS // DP
    table_out[...] = jnp.where(lax.rem(part, 2) == 0, mine[0:own, :], mine[own : 2 * own, :])

    def drain(c, carry):
        for copy in in_copies(*kv, c) + in_copies(*qd, c):
            copy.wait_send()
        for g in range(3):
            give_copy(g, c).wait_send()
            back_copy(g, c).wait_send()
        for a in range(3):
            for copy in ret_copies(a, c):
                copy.wait_send()
        return carry

    lax.fori_loop(0, CHUNKS, drain, 0)
    for j in range(1, DP):
        table_copy(j).wait_send()
        dp_copy(j).wait_send()
    for j in range(1, SIDE):
        entry_copy(j).wait_send()
    for j in range(1, SEQ):
        seq_copy(j).wait_send()
    for a in range(3):
        arrived(outs[a], out_recv.at[a])


def per_device(queries, keys, values, grad_out, bias_table, slot_tiles, live, buckets):
    hbm = pl.BlockSpec(memory_space=pltpu.HBM)
    vmem = pl.BlockSpec(memory_space=pltpu.VMEM)
    smem = pl.BlockSpec(memory_space=pltpu.SMEM)
    low, full = jnp.bfloat16, jnp.float32
    dma = pltpu.SemaphoreType.DMA
    moved = [pltpu.VMEM((CHUNKS, 2, len(group), TILE, HEAD_DIM), low) for group, _ in GROUPS]
    set_rows = ENTRIES * TILE
    out = jax.ShapeDtypeStruct((TOK_DEV, WIDTH), low)
    result = pl.pallas_call(
        kernel,
        out_shape=(out, out, out, jax.ShapeDtypeStruct((HEADS // DP, TABLE), full)),
        in_specs=[hbm] * 4 + [vmem, smem, smem, smem],
        out_specs=(hbm, hbm, hbm, vmem),
        scratch_shapes=[
            pltpu.VMEM((CHUNKS, 2, SIDE, TOK_DEV, HEAD_DIM), low),
            pltpu.VMEM((CHUNKS, 2, SIDE, TOK_DEV, HEAD_DIM), low),
            *moved, *moved, *moved, *moved,
            pltpu.VMEM((CHUNKS, 3, SIDE, TOK_DEV, HEAD_DIM), low),
            pltpu.VMEM((2, 2, SIDE, TOK_DEV, HEAD_DIM), full),
            pltpu.VMEM((SIDE, set_rows, HEAD_DIM), low),
            pltpu.VMEM((SIDE, set_rows, HEAD_DIM), low),
            pltpu.VMEM((SIDE, set_rows, HEAD_DIM), full),
            pltpu.VMEM((SIDE, set_rows, HEAD_DIM), full),
            pltpu.VMEM((DP, 8, TABLE), full),
            pltpu.VMEM((SIDE, 2, 8, TABLE), full),
            pltpu.VMEM((TILE_COLS + TILE_ROWS, TABLE), full),
            pltpu.VMEM((TILE, 2 * TILE), full),
            pltpu.VMEM((TILE, TILE), full),
            pltpu.VMEM((8, TABLE), full),
            pltpu.VMEM((8, TABLE), full),
            pltpu.VMEM((DP, 8, TABLE), full),
            pltpu.VMEM((SEQ, 8, TABLE), full),
            dma((CHUNKS, 2, SIDE)), dma((CHUNKS,)),
            dma((CHUNKS, 2, SIDE)), dma((CHUNKS,)),
            dma((CHUNKS, 3)), dma((CHUNKS, 3)),
            dma((CHUNKS, 3)), dma((CHUNKS, 3)),
            dma((CHUNKS, 3, SIDE)), dma((3,)),
            dma((DP,)), dma((DP,)),
            dma((SIDE,)), dma((SIDE,)),
            dma((DP,)), dma((DP,)),
            dma((SEQ,)), dma((SEQ,)),
        ],
        compiler_params=pltpu.CompilerParams(
            collective_id=0, has_side_effects=True, vmem_limit_bytes=60 * 2**20
        ),
        cost_estimate=pl.CostEstimate(
            flops=7_046_430_720, bytes_accessed=11_000_000, transcendentals=5_505_024
        ),
    )(queries[0], keys[0], values[0], grad_out[0], bias_table, slot_tiles, live, buckets)
    query_grad, key_grad, value_grad, table_grad = result
    return (query_grad[None], key_grad[None], value_grad[None], table_grad)


def solution(mesh):
    rows = P("dp", "seq", None)
    return jax.shard_map(
        per_device,
        mesh=mesh,
        in_specs=(rows, rows, rows, rows, P("dp", None), P(), P("seq", None), P("seq", None)),
        out_specs=(rows, rows, rows, P("dp", None)),
        check_vma=False,
    )
```

time: 483 us -> 157 us (0.33); the launches traced: 474 us -> 157 us
  Pallas kernels: 0 us -> 148 us
  matrix products: 133 us -> 0 us
  blocking collectives: 112 us -> 0 us
  local copies, waits for them, and re-layouts: 116 us -> 7.83 us
  starting transfers between devices: 46.1 us -> 0 us
  other arithmetic: 40.5 us -> 0 us
  waiting for transfers between devices: 15.4 us -> 0 us
  loops' own time: 5.82 us -> 0 us
    pallas_call x0 -> x1, Pallas kernels: none -> 148 us  [per_device(): pl.pallas_call(kernel, out_shape=(out, out, out, jax.ShapeDtypeStruct((HE...]
    dot_general x55 -> x0, matrix products: 133 us -> none  [the longest x14 48.7 us: products_of(): jnp.einsum('qhd,khd->hqk', upstream_heads, value_heads, preferred_element...]
    psum x1 -> x0, blocking collectives: 73.2 us -> none  [per_device(): summed = lax.psum(table_grad, 'seq')]
    ppermute x10 -> x0, starting transfers between devices: 46.1 us -> none  [the longest x8 35.2 us: from_behind(): return lax.ppermute(block, axis, route)]
    slice x19 -> x0, local copies, waits for them, and re-layouts: 30.6 us -> none  [the longest x14 30.5 us: products_of(): value_heads = pair[1].reshape(TILE, HEADS, HEAD_DIM)]
    while x117 -> x0, local copies, waits for them, and re-layouts: 28 us -> none
    unnamed x1 -> x0, blocking collectives: 25.6 us -> none
    unnamed x46 -> x11, local copies, waits for them, and re-layouts: 32.6 us -> 7.83 us
  transfers between devices with their start and end apart: 10 -> 0, of which waited for: 1 -> 0; matrix products, arithmetic and copies ran while one was open for 18% -> 0% of each run, Pallas kernels for 0% -> 0%
where the time goes in v1:
time: 157 us
  Pallas kernels  148 us (94%)
  local copies, waits for them, and re-layouts  7.83 us (5%)
    pallas_call x1, Pallas kernels, per_device(): pl.pallas_call(kernel, out_shape=(out, out, out, jax.ShapeDtypeStruct((HE...  148 us
    unnamed x11, local copies, waits for them, and re-layouts  7.83 us

profile of v1, /device:TPU:0, one launch (start us, length us, event | category | flops | bytes accessed | tf_op | source)
XLA Modules:
  0.0 156.8 jit_solution(855743513964702987)
XLA Ops:
  0.6 1.4 copy.12.slots
  2.0 148.3 %shard_map.111 = (bf16[256,3072]{1,0:T(8,128)(2,1)}, bf16[256,3072]{1,0:T(8,128)(2,1)}, bf16[256,3072]{1,0:T(8,128)(2,1)}, f32[3,128]{1,0:T(4,128)}) custom-call(bf16[256,3072]{1,0:T(8,128)(2,1)} %bitcast.10, bf16[256,3072]{1,0:T(8,128)(2,1)} %bitcast.11, bf16[256,3072]{1,0:T(8,128)(2,1)} %bitcast.12, bf16[256,3072]{1,0:T(8,128)(2,1)} %bitcast.13, ...), custom_call_target="tpu_custom_call" | custom-call | flops 7046430720 | bytes 11000000 | tf_op jit(solution)/shard_map/pallas_call | solution.py:429
  150.3 0.0 copy-start.1
  150.3 2.8 %copy.17 = bf16[1,256,3072]{2,1,0:T(8,128)(2,1)} copy(bf16[1,256,3072]{2,1,0:T(8,128)(2,1)} %bitcast.9) | data formatting | bytes 3145728
  153.0 0.0 copy-done.1
  153.1 0.0 copy-start
  153.1 1.1 copy.18
  154.2 0.8 copy-done
  155.0 0.0 copy-start.2
  155.0 1.1 copy.19
  156.2 0.0 copy-done.2
  156.2 0.6 copy.20
Async XLA Ops:
  150.3 2.8 %copy-start.1 = (bf16[256,3072]{1,0:T(8,128)(2,1)S(1)}, bf16[256,3072]{1,0:T(8,128)(2,1)}, u32[]{:S(2)}) copy-start(bf16[256,3072]{1,0:T(8,128)(2,1)} %get-tuple-element.9) | copy-start | bytes 4718596
  153.1 2.0 %copy-start = (bf16[256,3072]{1,0:T(8,128)(2,1)S(1)}, bf16[256,3072]{1,0:T(8,128)(2,1)}, u32[]{:S(2)}) copy-start(bf16[256,3072]{1,0:T(8,128)(2,1)} %get-tuple-element.10) | copy-start | bytes 4718596
  155.0 1.1 copy-start.2

commit v2 on v1

--- a/solution.py
+++ b/solution.py
@@ -43,11 +43,13 @@
 
 
 def kernel(
-    queries, keys, values, upstream, table, slots, live, buckets,
+    queries, keys, values, upstream, table, slots_hbm, live_hbm, buckets_hbm,
     query_out, key_out, value_out, table_out,
     kv_in, qd_in, give0, give1, give2, got0, got1, got2, back0, back1, back2, home0, home1, home2,
     ret, acc, key_set, value_set, key_part, value_part,
+    slots, live, buckets, own_heads, direct,
     tables, entries, shifted, fine, fine_sum, coarse_sum, grads, grads_dp, grads_seq,
+    small_recv, own_recv,
     kv_send, kv_recv, qd_send, qd_recv, give_send, got_recv, back_send, home_recv, ret_send, out_recv,
     table_send, table_recv, entry_send, entry_recv, dp_send, dp_recv, seq_send, seq_recv,
 ):
@@ -82,6 +84,25 @@
         pl.semaphore_signal(
             barrier, inc=1, device_id={"dp": lax.rem(part + j, DP)}, device_id_type=MESH
         )
+
+    small = [
+        pltpu.make_async_copy(source, target, small_recv.at[n])
+        for n, (source, target) in enumerate(
+            ((slots_hbm, slots), (live_hbm, live), (buckets_hbm, buckets))
+        )
+    ]
+    for copy in small:
+        copy.start()
+    for a, ref in enumerate((keys, values)):
+        for to in range(SIDE):
+            pltpu.make_async_copy(
+                ref.at[:, head_columns(to * CHUNKS)], own_heads.at[a, to], own_recv
+            ).start()
+    for copy in small:
+        copy.wait()
+
+    def upper(query_row, q, s):
+        return lax.rem(slots[s, lax.rem(query_row, SIDE) * SIDE + q], TILES_DEV) == 1
 
     lane = iota((8, TABLE), 1)
     row = iota((8, TABLE), 0)
@@ -95,6 +116,13 @@
     entries[x, 0] = (lane == bucket).astype(jnp.float32)
     entries[x, 1] = jnp.where(alive > 0, 0.0, NEGATIVE)
     grads[...] = jnp.zeros_like(grads)
+    arrived(own_heads, own_recv)
+    half_pick = upper(y + SIDE // 2, x, SLOTS - 1)
+    for a in range(2):
+        for to in range(SIDE):
+            direct[a, to] = jnp.where(
+                half_pick, own_heads[a, to, TILE : 2 * TILE, :], own_heads[a, to, 0:TILE, :]
+            )
 
     pl.semaphore_wait(barrier, SEQ - 1 + DP - 1)
 
@@ -109,101 +137,88 @@
             entries.at[x], entries.at[x], entry_send.at[j], entry_recv.at[x], seq_at(x + j, y)
         )
 
-    def in_copies(refs, buffer, send, recv, c):
-        copies = []
+    def fetch(refs, buffer, send, recv, c):
         for a, ref in enumerate(refs):
-            for j in range(1, SIDE):
+            for j in (2, 1, 3):
                 to = lax.rem(x + j, SIDE)
-                copies.append(
-                    remote(
-                        ref.at[:, head_columns(to * CHUNKS + c)], buffer.at[c, a, x],
-                        send.at[c, a, j], recv.at[c], seq_at(to, y),
-                    )
-                )
-        return copies
-
-    def fetch(refs, buffer, send, recv, c):
-        for copy in in_copies(refs, buffer, send, recv, c):
-            copy.start()
-        for a, ref in enumerate(refs):
+                remote(
+                    ref.at[:, head_columns(to * CHUNKS + c)], buffer.at[c, a, x],
+                    send, recv.at[c, a], seq_at(to, y),
+                ).start()
             pltpu.make_async_copy(
-                ref.at[:, head_columns(x * CHUNKS + c)], buffer.at[c, a, x], recv.at[c]
+                ref.at[:, head_columns(x * CHUNKS + c)], buffer.at[c, a, x], recv.at[c, a]
             ).start()
 
     kv = ((keys, values), kv_in, kv_send, kv_recv)
     qd = ((queries, upstream), qd_in, qd_send, qd_recv)
 
-    def give_copy(g, c):
+    def give_copy(g, c, a):
         return remote(
-            gives[g].at[c], gots[g].at[c], give_send.at[c, g], got_recv.at[c, g],
+            gives[g].at[c, a], gots[g].at[c, a], give_send.at[g], got_recv.at[c, g, a],
             seq_at(x, y + GROUPS[g][1]),
         )
 
-    def back_copy(g, c):
+    def back_copy(g, c, a):
         return remote(
-            backs[g].at[c], homes[g].at[c], back_send.at[c, g], home_recv.at[c, g],
+            backs[g].at[c, a], homes[g].at[c, a], back_send.at[g], home_recv.at[c, g, a],
             seq_at(x, y + SIDE - GROUPS[g][1]),
         )
 
-    def ret_copies(a, c):
-        return [
+    def give_back(a, c):
+        columns = head_columns(x * CHUNKS + c)
+        for j in (2, 1, 3):
             remote(
-                ret.at[c, a, lax.rem(x + j, SIDE)], outs[a].at[:, head_columns(x * CHUNKS + c)],
-                ret_send.at[c, a, j], out_recv.at[a], seq_at(x + j, y),
-            )
-            for j in range(1, SIDE)
-        ]
-
-    def give_back(a, c):
-        for copy in ret_copies(a, c):
-            copy.start()
-        pltpu.make_async_copy(
-            ret.at[c, a, x], outs[a].at[:, head_columns(x * CHUNKS + c)], out_recv.at[a]
-        ).start()
-
-    def upper(query_row, q, s):
-        return lax.rem(slots[lax.rem(query_row, SIDE) * SIDE + q, s], TILES_DEV) == 1
-
+                ret.at[c, a, lax.rem(x + j, SIDE)], outs[a].at[:, columns],
+                ret_send.at[a], out_recv.at[a], seq_at(x + j, y),
+            ).start()
+        pltpu.make_async_copy(ret.at[c, a, x], outs[a].at[:, columns], out_recv.at[a]).start()
+
+    for a in range(2):
+        for to in range(SIDE):
+            remote(
+                direct.at[a, to], gots[2].at[0, a, x], give_send.at[2], got_recv.at[0, 2, a],
+                seq_at(to, y + SIDE // 2),
+            ).start()
+    fetch(*kv, 0)
     for j in range(1, DP):
         table_copy(j).start()
     for j in range(1, SIDE):
         entry_copy(j).start()
-    fetch(*kv, 0)
+    fetch(*kv, 1)
     fetch(*qd, 0)
-    fetch(*kv, 1)
-    for j in range(1, DP):
-        source = lax.rem(part + j, DP)
-        arrived(tables.at[source], table_recv.at[source])
-    for j in range(1, SIDE):
-        source = lax.rem(x + j, SIDE)
-        arrived(entries.at[source], entry_recv.at[source])
 
     def halves(c, a, tile):
         return kv_in[c, a, tile, 0:TILE, :], kv_in[c, a, tile, TILE : 2 * TILE, :]
 
     def send_tiles(c):
-        arrived(kv_in.at[c], kv_recv.at[c])
+        for a in range(2):
+            arrived(kv_in.at[c, a], kv_recv.at[c, a])
+            for g, (group, distance) in enumerate(GROUPS):
+
+                def give(g=g, group=group, distance=distance):
+                    for n, (q, s, tile) in enumerate(group):
+                        low, high = halves(c, a, tile)
+                        gives[g][c, a, n] = jnp.where(upper(y + distance, q, s), high, low)
+                    give_copy(g, c, a).start()
+
+                if g < 2:
+                    give()
+                else:
+                    pl.when(c > 0)(give)
+
+        @pl.when(c + 2 < CHUNKS)
+        def _():
+            fetch(*kv, c + 2)
 
         @pl.when(c + 1 < CHUNKS)
         def _():
             fetch(*qd, c + 1)
 
-        @pl.when(c + 2 < CHUNKS)
-        def _():
-            fetch(*kv, c + 2)
-
-        for g, (group, distance) in enumerate(GROUPS):
-            for n, (q, s, tile) in enumerate(group):
-                pick = upper(y + distance, q, s)
-                for a in range(2):
-                    low, high = halves(c, a, tile)
-                    gives[g][c, a, n] = jnp.where(pick, high, low)
-            give_copy(g, c).start()
-
     def compute(c):
-        arrived(qd_in.at[c], qd_recv.at[c])
-        for g in range(3):
-            arrived(gots[g].at[c], got_recv.at[c, g])
+        for a in range(2):
+            arrived(qd_in.at[c, a], qd_recv.at[c, a])
+            for g in range(3):
+                arrived(gots[g].at[c, a], got_recv.at[c, g, a])
         sets = (key_set, value_set)
         for a in range(2):
             for q in range(SIDE):
@@ -294,12 +309,12 @@
         lax.fori_loop(0, SIDE, one_query_tile, 0)
         give_back(0, c)
         parts = (key_part, value_part)
-        for g, (group, _) in enumerate(GROUPS):
-            for n, (q, s, _) in enumerate(group):
-                at = (TILES_DEV + s) * TILE
-                for a in range(2):
+        for a in range(2):
+            for g, (group, _) in enumerate(GROUPS):
+                for n, (q, s, _) in enumerate(group):
+                    at = (TILES_DEV + s) * TILE
                     backs[g][c, a, n] = parts[a][q, at : at + TILE, :].astype(jnp.bfloat16)
-            back_copy(g, c).start()
+                back_copy(g, c, a).start()
         slot = lax.rem(c, 2)
         for a in range(2):
             for q in range(SIDE):
@@ -333,13 +348,14 @@
 
     def finish(c):
         slot = lax.rem(c, 2)
-        for g, (group, distance) in enumerate(GROUPS):
-            arrived(homes[g].at[c], home_recv.at[c, g])
-            for n, (q, s, tile) in enumerate(group):
-                pick = upper(y + distance, q, s)
-                for a in range(2):
-                    deposit(slot, a, tile, pick, homes[g][c, a, n].astype(jnp.float32))
         for a in range(2):
+            for g, (group, distance) in enumerate(GROUPS):
+                arrived(homes[g].at[c, a], home_recv.at[c, g, a])
+                for n, (q, s, tile) in enumerate(group):
+                    deposit(
+                        slot, a, tile, upper(y + distance, q, s),
+                        homes[g][c, a, n].astype(jnp.float32),
+                    )
             for q in range(SIDE):
                 ret[c, 1 + a, q] = acc[slot, a, q].astype(jnp.bfloat16)
             give_back(1 + a, c)
@@ -361,7 +377,16 @@
         def _():
             send_tiles(t)
 
-        @pl.when((t >= 1) & (t < CHUNKS + 1))
+        @pl.when(t == 1)
+        def _():
+            for j in range(1, DP):
+                source = lax.rem(part + j, DP)
+                arrived(tables.at[source], table_recv.at[source])
+            for j in range(1, SIDE):
+                source = lax.rem(x + j, SIDE)
+                arrived(entries.at[source], entry_recv.at[source])
+
+        @pl.when(t >= 1)
         def _():
             compute(t - 1)
 
@@ -394,18 +419,14 @@
     own = HEADS // DP
     table_out[...] = jnp.where(lax.rem(part, 2) == 0, mine[0:own, :], mine[own : 2 * own, :])
 
-    def drain(c, carry):
-        for copy in in_copies(*kv, c) + in_copies(*qd, c):
-            copy.wait_send()
-        for g in range(3):
-            give_copy(g, c).wait_send()
-            back_copy(g, c).wait_send()
-        for a in range(3):
-            for copy in ret_copies(a, c):
-                copy.wait_send()
-        return carry
-
-    lax.fori_loop(0, CHUNKS, drain, 0)
+    peers = slice(0, SIDE - 1)
+    arrived(kv_in.at[:, :, peers], kv_send)
+    arrived(qd_in.at[:, :, peers], qd_send)
+    for g in range(3):
+        arrived(gives[g], give_send.at[g])
+        arrived(backs[g], back_send.at[g])
+    for a in range(3):
+        arrived(ret.at[:, a, peers], ret_send.at[a])
     for j in range(1, DP):
         table_copy(j).wait_send()
         dp_copy(j).wait_send()
@@ -420,7 +441,6 @@
 def per_device(queries, keys, values, grad_out, bias_table, slot_tiles, live, buckets):
     hbm = pl.BlockSpec(memory_space=pltpu.HBM)
     vmem = pl.BlockSpec(memory_space=pltpu.VMEM)
-    smem = pl.BlockSpec(memory_space=pltpu.SMEM)
     low, full = jnp.bfloat16, jnp.float32
     dma = pltpu.SemaphoreType.DMA
     moved = [pltpu.VMEM((CHUNKS, 2, len(group), TILE, HEAD_DIM), low) for group, _ in GROUPS]
@@ -429,7 +449,7 @@
     result = pl.pallas_call(
         kernel,
         out_shape=(out, out, out, jax.ShapeDtypeStruct((HEADS // DP, TABLE), full)),
-        in_specs=[hbm] * 4 + [vmem, smem, smem, smem],
+        in_specs=[hbm] * 4 + [vmem, hbm, hbm, hbm],
         out_specs=(hbm, hbm, hbm, vmem),
         scratch_shapes=[
             pltpu.VMEM((CHUNKS, 2, SIDE, TOK_DEV, HEAD_DIM), low),
@@ -441,6 +461,11 @@
             pltpu.VMEM((SIDE, set_rows, HEAD_DIM), low),
             pltpu.VMEM((SIDE, set_rows, HEAD_DIM), full),
             pltpu.VMEM((SIDE, set_rows, HEAD_DIM), full),
+            pltpu.SMEM((SLOTS, SEQ), jnp.int32),
+            pltpu.SMEM(live.shape, jnp.int32),
+            pltpu.SMEM(buckets.shape, jnp.int32),
+            pltpu.VMEM((2, SIDE, TOK_DEV, HEAD_DIM), low),
+            pltpu.VMEM((2, SIDE, TILE, HEAD_DIM), low),
             pltpu.VMEM((DP, 8, TABLE), full),
             pltpu.VMEM((SIDE, 2, 8, TABLE), full),
             pltpu.VMEM((TILE_COLS + TILE_ROWS, TABLE), full),
@@ -450,11 +475,12 @@
             pltpu.VMEM((8, TABLE), full),
             pltpu.VMEM((DP, 8, TABLE), full),
             pltpu.VMEM((SEQ, 8, TABLE), full),
-            dma((CHUNKS, 2, SIDE)), dma((CHUNKS,)),
-            dma((CHUNKS, 2, SIDE)), dma((CHUNKS,)),
-            dma((CHUNKS, 3)), dma((CHUNKS, 3)),
-            dma((CHUNKS, 3)), dma((CHUNKS, 3)),
-            dma((CHUNKS, 3, SIDE)), dma((3,)),
+            dma((3,)), dma(()),
+            dma(()), dma((CHUNKS, 2)),
+            dma(()), dma((CHUNKS, 2)),
+            dma((3,)), dma((CHUNKS, 3, 2)),
+            dma((3,)), dma((CHUNKS, 3, 2)),
+            dma((3,)), dma((3,)),
             dma((DP,)), dma((DP,)),
             dma((SIDE,)), dma((SIDE,)),
             dma((DP,)), dma((DP,)),
@@ -466,7 +492,7 @@
         cost_estimate=pl.CostEstimate(
             flops=7_046_430_720, bytes_accessed=11_000_000, transcendentals=5_505_024
         ),
-    )(queries[0], keys[0], values[0], grad_out[0], bias_table, slot_tiles, live, buckets)
+    )(queries[0], keys[0], values[0], grad_out[0], bias_table, slot_tiles.T, live, buckets)
     query_grad, key_grad, value_grad, table_grad = result
     return (query_grad[None], key_grad[None], value_grad[None], table_grad)
 

time: 157 us -> 152 us (0.968)
  Pallas kernels: 148 us -> 144 us
    pallas_call x1, Pallas kernels: 148 us -> 144 us  [per_device(): pl.pallas_call(kernel, out_shape=(out, out, out, jax.ShapeDtypeStruct((HE...]
    unnamed x11 -> x10, local copies, waits for them, and re-layouts: 7.83 us -> 6.47 us
where the time goes in v2:
time: 152 us; the launch traced here: 151 us
  Pallas kernels  144 us (95%)
  local copies, waits for them, and re-layouts  6.47 us (4%)
    pallas_call x1, Pallas kernels, per_device(): pl.pallas_call(kernel, out_shape=(out, out, out, jax.ShapeDtypeStruct((HE...  144 us
    unnamed x10, local copies, waits for them, and re-layouts  6.47 us

profile of v2, /device:TPU:0, one launch (start us, length us, event | category | flops | bytes accessed | tf_op | source)
XLA Modules:
  0.0 151.2 jit_solution(8441398846629437320)
XLA Ops:
  0.6 144.0 %shard_map.111 = (bf16[256,3072]{1,0:T(8,128)(2,1)}, bf16[256,3072]{1,0:T(8,128)(2,1)}, bf16[256,3072]{1,0:T(8,128)(2,1)}, f32[3,128]{1,0:T(4,128)}) custom-call(bf16[256,3072]{1,0:T(8,128)(2,1)} %bitcast.11, bf16[256,3072]{1,0:T(8,128)(2,1)} %bitcast.12, bf16[256,3072]{1,0:T(8,128)(2,1)} %bitcast.13, bf16[256,3072]{1,0:T(8,128)(2,1)} %bitcast.14, ...), custom_call_target="tpu_custom_call" | custom-call | flops 7046430720 | bytes 11000000 | tf_op jit(solution)/shard_map/pallas_call | solution.py:449
  144.7 0.0 copy-start.1
  144.7 2.8 %copy.16 = bf16[1,256,3072]{2,1,0:T(8,128)(2,1)} copy(bf16[1,256,3072]{2,1,0:T(8,128)(2,1)} %bitcast.10) | data formatting | bytes 3145728
  147.5 0.0 copy-done.1
  147.5 0.0 copy-start
  147.5 1.1 copy.17
  148.6 0.8 copy-done
  149.4 0.0 copy-start.2
  149.4 1.1 copy.18
  150.6 0.0 copy-done.2
  150.6 0.6 copy.19
Async XLA Ops:
  144.7 2.8 %copy-start.1 = (bf16[256,3072]{1,0:T(8,128)(2,1)S(1)}, bf16[256,3072]{1,0:T(8,128)(2,1)}, u32[]{:S(2)}) copy-start(bf16[256,3072]{1,0:T(8,128)(2,1)} %get-tuple-element.9) | copy-start | bytes 4718596
  147.5 2.0 %copy-start = (bf16[256,3072]{1,0:T(8,128)(2,1)S(1)}, bf16[256,3072]{1,0:T(8,128)(2,1)}, u32[]{:S(2)}) copy-start(bf16[256,3072]{1,0:T(8,128)(2,1)} %get-tuple-element.10) | copy-start | bytes 4718596
  149.4 1.1 copy-start.2

commit v3 on v2

--- a/solution.py
+++ b/solution.py
@@ -29,6 +29,8 @@
 HIGHEST = lax.Precision.HIGHEST
 MESH = pl.DeviceIdType.MESH
 
+ORDER = (2, 1, 3, 0)
+
 FROM_BELOW = tuple((q, s, q + o + SIDE) for q in range(SIDE) for s, o in enumerate(NEAR_OFFSETS) if q + o < 0)
 FROM_ABOVE = tuple((q, s, q + o - SIDE) for q in range(SIDE) for s, o in enumerate(NEAR_OFFSETS) if q + o >= SIDE)
 FROM_HALF = tuple((q, SLOTS - 1, q) for q in range(SIDE))
@@ -47,10 +49,10 @@
     query_out, key_out, value_out, table_out,
     kv_in, qd_in, give0, give1, give2, got0, got1, got2, back0, back1, back2, home0, home1, home2,
     ret, acc, key_set, value_set, key_part, value_part,
-    slots, live, buckets, own_heads, direct,
+    slots, live, buckets, own_heads, direct, own_later, later,
     tables, entries, shifted, fine, fine_sum, coarse_sum, grads, grads_dp, grads_seq,
-    small_recv, own_recv,
-    kv_send, kv_recv, qd_send, qd_recv, give_send, got_recv, back_send, home_recv, ret_send, out_recv,
+    small_recv, own_recv, later_recv,
+    kv_send, kv_recv, qd_send, qd_recv, give_send, got_recv, back_send, home_recv, far_recv, ret_send, out_recv,
     table_send, table_recv, entry_send, entry_recv, dp_send, dp_recv, seq_send, seq_recv,
 ):
     gives, gots = (give0, give1, give2), (got0, got1, got2)
@@ -97,6 +99,10 @@
         for to in range(SIDE):
             pltpu.make_async_copy(
                 ref.at[:, head_columns(to * CHUNKS)], own_heads.at[a, to], own_recv
+            ).start()
+        for c in range(1, CHUNKS):
+            pltpu.make_async_copy(
+                ref.at[:, head_columns(x * CHUNKS + c)], own_later.at[a, c - 1], later_recv
             ).start()
     for copy in small:
         copy.wait()
@@ -123,6 +129,12 @@
             direct[a, to] = jnp.where(
                 half_pick, own_heads[a, to, TILE : 2 * TILE, :], own_heads[a, to, 0:TILE, :]
             )
+    arrived(own_later, later_recv)
+    for a in range(2):
+        for c in range(CHUNKS - 1):
+            later[a, c] = jnp.where(
+                half_pick, own_later[a, c, TILE : 2 * TILE, :], own_later[a, c, 0:TILE, :]
+            )
 
     pl.semaphore_wait(barrier, SEQ - 1 + DP - 1)
 
@@ -139,7 +151,7 @@
 
     def fetch(refs, buffer, send, recv, c):
         for a, ref in enumerate(refs):
-            for j in (2, 1, 3):
+            for j in ORDER[:-1]:
                 to = lax.rem(x + j, SIDE)
                 remote(
                     ref.at[:, head_columns(to * CHUNKS + c)], buffer.at[c, a, x],
@@ -164,14 +176,21 @@
             seq_at(x, y + SIDE - GROUPS[g][1]),
         )
 
-    def give_back(a, c):
+    def far_back(c, a, tile):
+        return remote(
+            backs[2].at[c, a, tile], homes[2].at[c, a, tile], back_send.at[2],
+            far_recv.at[c, a, tile], seq_at(x, y + SIDE // 2),
+        )
+
+    def give_back(a, c, j):
         columns = head_columns(x * CHUNKS + c)
-        for j in (2, 1, 3):
+        source = ret.at[c, a, lax.rem(x + j, SIDE)]
+        if j == 0:
+            pltpu.make_async_copy(source, outs[a].at[:, columns], out_recv.at[a]).start()
+        else:
             remote(
-                ret.at[c, a, lax.rem(x + j, SIDE)], outs[a].at[:, columns],
-                ret_send.at[a], out_recv.at[a], seq_at(x + j, y),
+                source, outs[a].at[:, columns], ret_send.at[a], out_recv.at[a], seq_at(x + j, y)
             ).start()
-        pltpu.make_async_copy(ret.at[c, a, x], outs[a].at[:, columns], out_recv.at[a]).start()
 
     for a in range(2):
         for to in range(SIDE):
@@ -180,11 +199,18 @@
                 seq_at(to, y + SIDE // 2),
             ).start()
     fetch(*kv, 0)
+    for c in range(1, CHUNKS):
+        for a in range(2):
+            remote(
+                later.at[a, c - 1], gots[2].at[c, a, x], give_send.at[2], got_recv.at[c, 2, a],
+                seq_at(x, y + SIDE // 2),
+            ).start()
     for j in range(1, DP):
         table_copy(j).start()
     for j in range(1, SIDE):
         entry_copy(j).start()
     fetch(*kv, 1)
+    fetch(*kv, 2)
     fetch(*qd, 0)
 
     def halves(c, a, tile):
@@ -193,22 +219,27 @@
     def send_tiles(c):
         for a in range(2):
             arrived(kv_in.at[c, a], kv_recv.at[c, a])
-            for g, (group, distance) in enumerate(GROUPS):
-
-                def give(g=g, group=group, distance=distance):
-                    for n, (q, s, tile) in enumerate(group):
-                        low, high = halves(c, a, tile)
-                        gives[g][c, a, n] = jnp.where(upper(y + distance, q, s), high, low)
-                    give_copy(g, c, a).start()
-
-                if g < 2:
-                    give()
-                else:
-                    pl.when(c > 0)(give)
-
-        @pl.when(c + 2 < CHUNKS)
-        def _():
-            fetch(*kv, c + 2)
+            for g, (group, distance) in enumerate(GROUPS[:2]):
+                for n, (q, s, tile) in enumerate(group):
+                    low, high = halves(c, a, tile)
+                    gives[g][c, a, n] = jnp.where(upper(y + distance, q, s), high, low)
+                give_copy(g, c, a).start()
+
+            @pl.when(c > 0)
+            def _():
+                for j in ORDER[:-1]:
+                    tile = lax.rem(x + j, SIDE)
+                    low, high = halves(c, a, tile)
+                    pick = upper(y + SIDE // 2, tile, SLOTS - 1)
+                    gives[2][c, a, tile] = jnp.where(pick, high, low)
+                    remote(
+                        gives[2].at[c, a, tile], gots[2].at[c, a, tile], give_send.at[2],
+                        got_recv.at[c, 2, a], seq_at(x, y + SIDE // 2),
+                    ).start()
+
+        @pl.when(c + 3 < CHUNKS)
+        def _():
+            fetch(*kv, c + 3)
 
         @pl.when(c + 1 < CHUNKS)
         def _():
@@ -307,14 +338,26 @@
             return carry
 
         lax.fori_loop(0, SIDE, one_query_tile, 0)
-        give_back(0, c)
+        for j in ORDER:
+            give_back(0, c, j)
         parts = (key_part, value_part)
-        for a in range(2):
-            for g, (group, _) in enumerate(GROUPS):
+
+        def return_far(c, a, j):
+            tile = lax.rem(x + j, SIDE)
+            at = (ENTRIES - 1) * TILE
+            backs[2][c, a, tile] = parts[a][tile, at : at + TILE, :].astype(jnp.bfloat16)
+            far_back(c, a, tile).start()
+
+        for a in range(2):
+            for g, (group, _) in enumerate(GROUPS[:2]):
                 for n, (q, s, _) in enumerate(group):
                     at = (TILES_DEV + s) * TILE
                     backs[g][c, a, n] = parts[a][q, at : at + TILE, :].astype(jnp.bfloat16)
                 back_copy(g, c, a).start()
+            for j in ORDER[:-1]:
+                return_far(c, a, j)
+        for a in range(2):
+            return_far(c, a, 0)
         slot = lax.rem(c, 2)
         for a in range(2):
             for q in range(SIDE):
@@ -346,19 +389,31 @@
         acc[slot, a, tile, 0:TILE, :] += jnp.where(pick, 0.0, partial)
         acc[slot, a, tile, TILE : 2 * TILE, :] += jnp.where(pick, partial, 0.0)
 
+    def finish_tile(c, a, j):
+        slot = lax.rem(c, 2)
+        tile = lax.rem(x + j, SIDE)
+        arrived(homes[2].at[c, a, tile], far_recv.at[c, a, tile])
+        deposit(
+            slot, a, tile, upper(y + SIDE // 2, tile, SLOTS - 1),
+            homes[2][c, a, tile].astype(jnp.float32),
+        )
+        ret[c, 1 + a, tile] = acc[slot, a, tile].astype(jnp.bfloat16)
+        give_back(1 + a, c, j)
+
     def finish(c):
         slot = lax.rem(c, 2)
         for a in range(2):
-            for g, (group, distance) in enumerate(GROUPS):
+            for g, (group, distance) in enumerate(GROUPS[:2]):
                 arrived(homes[g].at[c, a], home_recv.at[c, g, a])
                 for n, (q, s, tile) in enumerate(group):
                     deposit(
                         slot, a, tile, upper(y + distance, q, s),
                         homes[g][c, a, n].astype(jnp.float32),
                     )
-            for q in range(SIDE):
-                ret[c, 1 + a, q] = acc[slot, a, q].astype(jnp.bfloat16)
-            give_back(1 + a, c)
+            for j in ORDER[:-1]:
+                finish_tile(c, a, j)
+        for a in range(2):
+            finish_tile(c, a, 0)
 
     def dp_copy(j):
         return remote(
@@ -386,20 +441,23 @@
                 source = lax.rem(x + j, SIDE)
                 arrived(entries.at[source], entry_recv.at[source])
 
-        @pl.when(t >= 1)
-        def _():
-            compute(t - 1)
-
         @pl.when(t >= 2)
         def _():
-            finish(t - 2)
+            compute(t - 2)
+
+        @pl.when(t == CHUNKS + 1)
+        def _():
+            for j in range(1, DP):
+                dp_copy(j).start()
+
+        @pl.when(t >= 3)
+        def _():
+            finish(t - 3)
 
         return carry
 
-    lax.fori_loop(0, CHUNKS + 1, step, 0)
-
-    for j in range(1, DP):
-        dp_copy(j).start()
+    lax.fori_loop(0, CHUNKS + 2, step, 0)
+
     total = grads[...]
     for j in range(1, DP):
         source = lax.rem(part + j, DP)
@@ -466,6 +524,8 @@
             pltpu.SMEM(buckets.shape, jnp.int32),
             pltpu.VMEM((2, SIDE, TOK_DEV, HEAD_DIM), low),
             pltpu.VMEM((2, SIDE, TILE, HEAD_DIM), low),
+            pltpu.VMEM((2, CHUNKS - 1, TOK_DEV, HEAD_DIM), low),
+            pltpu.VMEM((2, CHUNKS - 1, TILE, HEAD_DIM), low),
             pltpu.VMEM((DP, 8, TABLE), full),
             pltpu.VMEM((SIDE, 2, 8, TABLE), full),
             pltpu.VMEM((TILE_COLS + TILE_ROWS, TABLE), full),
@@ -475,11 +535,11 @@
             pltpu.VMEM((8, TABLE), full),
             pltpu.VMEM((DP, 8, TABLE), full),
             pltpu.VMEM((SEQ, 8, TABLE), full),
-            dma((3,)), dma(()),
+            dma((3,)), dma(()), dma(()),
             dma(()), dma((CHUNKS, 2)),
             dma(()), dma((CHUNKS, 2)),
             dma((3,)), dma((CHUNKS, 3, 2)),
-            dma((3,)), dma((CHUNKS, 3, 2)),
+            dma((3,)), dma((CHUNKS, 2, 2)), dma((CHUNKS, 2, SIDE)),
             dma((3,)), dma((3,)),
             dma((DP,)), dma((DP,)),
             dma((SIDE,)), dma((SIDE,)),

time: 152 us -> 142 us (0.934)
  Pallas kernels: 144 us -> 135 us
    pallas_call x1, Pallas kernels: 144 us -> 135 us  [per_device(): pl.pallas_call(kernel, out_shape=(out, out, out, jax.ShapeDtypeStruct((HE...]
where the time goes in v3:
time: 142 us
  Pallas kernels  135 us (95%)
  local copies, waits for them, and re-layouts  6.47 us (5%)
    pallas_call x1, Pallas kernels, per_device(): pl.pallas_call(kernel, out_shape=(out, out, out, jax.ShapeDtypeStruct((HE...  135 us
    unnamed x10, local copies, waits for them, and re-layouts  6.47 us

profile of v3, /device:TPU:0, one launch (start us, length us, event | category | flops | bytes accessed | tf_op | source)
XLA Modules:
  0.0 141.6 jit_solution(10870781144710344873)
XLA Ops:
  0.6 134.5 %shard_map.111 = (bf16[256,3072]{1,0:T(8,128)(2,1)}, bf16[256,3072]{1,0:T(8,128)(2,1)}, bf16[256,3072]{1,0:T(8,128)(2,1)}, f32[3,128]{1,0:T(4,128)}) custom-call(bf16[256,3072]{1,0:T(8,128)(2,1)} %bitcast.11, bf16[256,3072]{1,0:T(8,128)(2,1)} %bitcast.12, bf16[256,3072]{1,0:T(8,128)(2,1)} %bitcast.13, bf16[256,3072]{1,0:T(8,128)(2,1)} %bitcast.14, ...), custom_call_target="tpu_custom_call" | custom-call | flops 7046430720 | bytes 11000000 | tf_op jit(solution)/shard_map/pallas_call | solution.py:507
  135.2 0.0 copy-start.1
  135.2 2.8 %copy.16 = bf16[1,256,3072]{2,1,0:T(8,128)(2,1)} copy(bf16[1,256,3072]{2,1,0:T(8,128)(2,1)} %bitcast.10) | data formatting | bytes 3145728
  137.9 0.0 copy-done.1
  137.9 0.0 copy-start
  137.9 1.1 copy.17
  139.1 0.8 copy-done
  139.9 0.0 copy-start.2
  139.9 1.1 copy.18
  141.1 0.0 copy-done.2
  141.1 0.6 copy.19
Async XLA Ops:
  135.2 2.8 %copy-start.1 = (bf16[256,3072]{1,0:T(8,128)(2,1)S(1)}, bf16[256,3072]{1,0:T(8,128)(2,1)}, u32[]{:S(2)}) copy-start(bf16[256,3072]{1,0:T(8,128)(2,1)} %get-tuple-element.9) | copy-start | bytes 4718596
  137.9 2.0 %copy-start = (bf16[256,3072]{1,0:T(8,128)(2,1)S(1)}, bf16[256,3072]{1,0:T(8,128)(2,1)}, u32[]{:S(2)}) copy-start(bf16[256,3072]{1,0:T(8,128)(2,1)} %get-tuple-element.10) | copy-start | bytes 4718596
  139.9 1.1 copy-start.2

commit v4 on v3

--- a/solution.py
+++ b/solution.py
@@ -22,6 +22,7 @@
 SIDE = 4
 SEQ = SIDE * SIDE
 DP = 8
+STRIDES = (1, 2, 4)
 CHUNKS = HEADS // SIDE
 NEGATIVE = -1e30
 SCALE = HEAD_DIM ** (-0.5)
@@ -45,13 +46,13 @@
 
 
 def kernel(
-    queries, keys, values, upstream, table, slots_hbm, live_hbm, buckets_hbm,
+    queries, keys, values, upstream, table_hbm, slots_hbm, live_hbm, buckets_hbm,
     query_out, key_out, value_out, table_out,
     kv_in, qd_in, give0, give1, give2, got0, got1, got2, back0, back1, back2, home0, home1, home2,
     ret, acc, key_set, value_set, key_part, value_part,
-    slots, live, buckets, own_heads, direct, own_later, later,
+    table, slots, live, buckets, own_heads, own_far,
     tables, entries, shifted, fine, fine_sum, coarse_sum, grads, grads_dp, grads_seq,
-    small_recv, own_recv, later_recv,
+    small_recv, own_recv,
     kv_send, kv_recv, qd_send, qd_recv, give_send, got_recv, back_send, home_recv, far_recv, ret_send, out_recv,
     table_send, table_recv, entry_send, entry_recv, dp_send, dp_recv, seq_send, seq_recv,
 ):
@@ -78,31 +79,24 @@
         return pl.ds(pl.multiple_of(head * HEAD_DIM, HEAD_DIM), HEAD_DIM)
 
     barrier = pltpu.get_barrier_semaphore()
-    for j in range(1, SEQ):
-        pl.semaphore_signal(
-            barrier, inc=1, device_id={"seq": lax.rem(place + j, SEQ)}, device_id_type=MESH
-        )
-    for j in range(1, DP):
-        pl.semaphore_signal(
-            barrier, inc=1, device_id={"dp": lax.rem(part + j, DP)}, device_id_type=MESH
-        )
-
+    pairs = tuple(part + o - 2 * o * lax.rem(lax.div(part, o), 2) for o in STRIDES)
+    greeted = [seq_at(x + j, y) for j in range(1, SIDE)]
+    greeted += [seq_at(x, y + j) for j in range(1, SIDE)]
+    greeted += [{"dp": pair} for pair in pairs]
+    for device in greeted:
+        pl.semaphore_signal(barrier, inc=1, device_id=device, device_id_type=MESH)
     small = [
         pltpu.make_async_copy(source, target, small_recv.at[n])
         for n, (source, target) in enumerate(
-            ((slots_hbm, slots), (live_hbm, live), (buckets_hbm, buckets))
+            ((slots_hbm, slots), (live_hbm, live), (buckets_hbm, buckets), (table_hbm, table))
         )
     ]
     for copy in small:
         copy.start()
     for a, ref in enumerate((keys, values)):
-        for to in range(SIDE):
+        for c in range(CHUNKS):
             pltpu.make_async_copy(
-                ref.at[:, head_columns(to * CHUNKS)], own_heads.at[a, to], own_recv
-            ).start()
-        for c in range(1, CHUNKS):
-            pltpu.make_async_copy(
-                ref.at[:, head_columns(x * CHUNKS + c)], own_later.at[a, c - 1], later_recv
+                ref.at[:, head_columns(x * CHUNKS + c)], own_heads.at[a, c], own_recv
             ).start()
     for copy in small:
         copy.wait()
@@ -125,24 +119,23 @@
     arrived(own_heads, own_recv)
     half_pick = upper(y + SIDE // 2, x, SLOTS - 1)
     for a in range(2):
-        for to in range(SIDE):
-            direct[a, to] = jnp.where(
-                half_pick, own_heads[a, to, TILE : 2 * TILE, :], own_heads[a, to, 0:TILE, :]
+        for c in range(CHUNKS):
+            own_far[a, c] = jnp.where(
+                half_pick, own_heads[a, c, TILE : 2 * TILE, :], own_heads[a, c, 0:TILE, :]
             )
-    arrived(own_later, later_recv)
-    for a in range(2):
-        for c in range(CHUNKS - 1):
-            later[a, c] = jnp.where(
-                half_pick, own_later[a, c, TILE : 2 * TILE, :], own_later[a, c, 0:TILE, :]
-            )
-
-    pl.semaphore_wait(barrier, SEQ - 1 + DP - 1)
-
-    def table_copy(j):
-        return remote(
-            tables.at[part], tables.at[part], table_send.at[j], table_recv.at[part],
-            {"dp": lax.rem(part + j, DP)},
-        )
+
+    pl.semaphore_wait(barrier, len(greeted))
+
+    def table_block(device, n):
+        stride = STRIDES[n]
+        return tables.at[pl.ds(lax.div(device, stride) * stride, stride)]
+
+    def table_copy(n):
+        block = table_block(part, n)
+        return remote(block, block, table_send.at[n], table_recv.at[n], {"dp": pairs[n]})
+
+    def table_arrived(n):
+        arrived(table_block(pairs[n], n), table_recv.at[n])
 
     def entry_copy(j):
         return remote(
@@ -192,26 +185,22 @@
                 source, outs[a].at[:, columns], ret_send.at[a], out_recv.at[a], seq_at(x + j, y)
             ).start()
 
-    for a in range(2):
-        for to in range(SIDE):
+    table_copy(0).start()
+    for j in range(1, SIDE):
+        entry_copy(j).start()
+    for c in range(CHUNKS):
+        for a in range(2):
             remote(
-                direct.at[a, to], gots[2].at[0, a, x], give_send.at[2], got_recv.at[0, 2, a],
-                seq_at(to, y + SIDE // 2),
-            ).start()
-    fetch(*kv, 0)
-    for c in range(1, CHUNKS):
-        for a in range(2):
-            remote(
-                later.at[a, c - 1], gots[2].at[c, a, x], give_send.at[2], got_recv.at[c, 2, a],
+                own_far.at[a, c], gots[2].at[c, a, x], give_send.at[2], got_recv.at[c, 2, a],
                 seq_at(x, y + SIDE // 2),
             ).start()
-    for j in range(1, DP):
-        table_copy(j).start()
-    for j in range(1, SIDE):
-        entry_copy(j).start()
+        if c == 0:
+            fetch(*kv, 0)
     fetch(*kv, 1)
     fetch(*kv, 2)
     fetch(*qd, 0)
+    table_arrived(0)
+    table_copy(1).start()
 
     def halves(c, a, tile):
         return kv_in[c, a, tile, 0:TILE, :], kv_in[c, a, tile, TILE : 2 * TILE, :]
@@ -225,17 +214,15 @@
                     gives[g][c, a, n] = jnp.where(upper(y + distance, q, s), high, low)
                 give_copy(g, c, a).start()
 
-            @pl.when(c > 0)
-            def _():
-                for j in ORDER[:-1]:
-                    tile = lax.rem(x + j, SIDE)
-                    low, high = halves(c, a, tile)
-                    pick = upper(y + SIDE // 2, tile, SLOTS - 1)
-                    gives[2][c, a, tile] = jnp.where(pick, high, low)
-                    remote(
-                        gives[2].at[c, a, tile], gots[2].at[c, a, tile], give_send.at[2],
-                        got_recv.at[c, 2, a], seq_at(x, y + SIDE // 2),
-                    ).start()
+            for j in ORDER[:-1]:
+                tile = lax.rem(x + j, SIDE)
+                low, high = halves(c, a, tile)
+                pick = upper(y + SIDE // 2, tile, SLOTS - 1)
+                gives[2][c, a, tile] = jnp.where(pick, high, low)
+                remote(
+                    gives[2].at[c, a, tile], gots[2].at[c, a, tile], give_send.at[2],
+                    got_recv.at[c, 2, a], seq_at(x, y + SIDE // 2),
+                ).start()
 
         @pl.when(c + 3 < CHUNKS)
         def _():
@@ -434,12 +421,15 @@
 
         @pl.when(t == 1)
         def _():
-            for j in range(1, DP):
-                source = lax.rem(part + j, DP)
-                arrived(tables.at[source], table_recv.at[source])
+            table_arrived(1)
+            table_copy(2).start()
             for j in range(1, SIDE):
                 source = lax.rem(x + j, SIDE)
                 arrived(entries.at[source], entry_recv.at[source])
+
+        @pl.when(t == 2)
+        def _():
+            table_arrived(2)
 
         @pl.when(t >= 2)
         def _():
@@ -485,8 +475,9 @@
         arrived(backs[g], back_send.at[g])
     for a in range(3):
         arrived(ret.at[:, a, peers], ret_send.at[a])
+    for n in range(len(STRIDES)):
+        table_copy(n).wait_send()
     for j in range(1, DP):
-        table_copy(j).wait_send()
         dp_copy(j).wait_send()
     for j in range(1, SIDE):
         entry_copy(j).wait_send()
@@ -503,12 +494,15 @@
     dma = pltpu.SemaphoreType.DMA
     moved = [pltpu.VMEM((CHUNKS, 2, len(group), TILE, HEAD_DIM), low) for group, _ in GROUPS]
     set_rows = ENTRIES * TILE
-    out = jax.ShapeDtypeStruct((TOK_DEV, WIDTH), low)
+    out = pltpu.VMEM((TOK_DEV, WIDTH), low)
+    operands = (
+        queries[0], keys[0], values[0], grad_out[0], bias_table, slot_tiles.T, live, buckets,
+    )
     result = pl.pallas_call(
         kernel,
         out_shape=(out, out, out, jax.ShapeDtypeStruct((HEADS // DP, TABLE), full)),
-        in_specs=[hbm] * 4 + [vmem, hbm, hbm, hbm],
-        out_specs=(hbm, hbm, hbm, vmem),
+        in_specs=[hbm] * len(operands),
+        out_specs=(vmem, vmem, vmem, vmem),
         scratch_shapes=[
             pltpu.VMEM((CHUNKS, 2, SIDE, TOK_DEV, HEAD_DIM), low),
             pltpu.VMEM((CHUNKS, 2, SIDE, TOK_DEV, HEAD_DIM), low),
@@ -519,13 +513,12 @@
             pltpu.VMEM((SIDE, set_rows, HEAD_DIM), low),
             pltpu.VMEM((SIDE, set_rows, HEAD_DIM), full),
             pltpu.VMEM((SIDE, set_rows, HEAD_DIM), full),
+            pltpu.VMEM(bias_table.shape, full),
             pltpu.SMEM((SLOTS, SEQ), jnp.int32),
             pltpu.SMEM(live.shape, jnp.int32),
             pltpu.SMEM(buckets.shape, jnp.int32),
-            pltpu.VMEM((2, SIDE, TOK_DEV, HEAD_DIM), low),
-            pltpu.VMEM((2, SIDE, TILE, HEAD_DIM), low),
-            pltpu.VMEM((2, CHUNKS - 1, TOK_DEV, HEAD_DIM), low),
-            pltpu.VMEM((2, CHUNKS - 1, TILE, HEAD_DIM), low),
+            pltpu.VMEM((2, CHUNKS, TOK_DEV, HEAD_DIM), low),
+            pltpu.VMEM((2, CHUNKS, TILE, HEAD_DIM), low),
             pltpu.VMEM((DP, 8, TABLE), full),
             pltpu.VMEM((SIDE, 2, 8, TABLE), full),
             pltpu.VMEM((TILE_COLS + TILE_ROWS, TABLE), full),
@@ -535,24 +528,24 @@
             pltpu.VMEM((8, TABLE), full),
             pltpu.VMEM((DP, 8, TABLE), full),
             pltpu.VMEM((SEQ, 8, TABLE), full),
-            dma((3,)), dma(()), dma(()),
+            dma((4,)), dma(()),
             dma(()), dma((CHUNKS, 2)),
             dma(()), dma((CHUNKS, 2)),
             dma((3,)), dma((CHUNKS, 3, 2)),
             dma((3,)), dma((CHUNKS, 2, 2)), dma((CHUNKS, 2, SIDE)),
             dma((3,)), dma((3,)),
-            dma((DP,)), dma((DP,)),
+            dma((len(STRIDES),)), dma((len(STRIDES),)),
             dma((SIDE,)), dma((SIDE,)),
             dma((DP,)), dma((DP,)),
             dma((SEQ,)), dma((SEQ,)),
         ],
         compiler_params=pltpu.CompilerParams(
-            collective_id=0, has_side_effects=True, vmem_limit_bytes=60 * 2**20
+            collective_id=0, has_side_effects=True, vmem_limit_bytes=48 * 2**20
         ),
         cost_estimate=pl.CostEstimate(
             flops=7_046_430_720, bytes_accessed=11_000_000, transcendentals=5_505_024
         ),
-    )(queries[0], keys[0], values[0], grad_out[0], bias_table, slot_tiles.T, live, buckets)
+    )(*[pltpu.with_memory_space_constraint(operand, pltpu.HBM) for operand in operands])
     query_grad, key_grad, value_grad, table_grad = result
     return (query_grad[None], key_grad[None], value_grad[None], table_grad)
 

time: 142 us -> 137 us (0.965)
  local copies, waits for them, and re-layouts: 6.47 us -> 4.01 us
  Pallas kernels: 135 us -> 133 us
    unnamed x10 -> x4, local copies, waits for them, and re-layouts: 6.47 us -> 4.01 us
    pallas_call x1, Pallas kernels: 135 us -> 133 us  [per_device(): pl.pallas_call(kernel, out_shape=(out, out, out, jax.ShapeDtypeStruct((HE...]
where the time goes in v4:
time: 137 us
  Pallas kernels  133 us (97%)
  local copies, waits for them, and re-layouts  4.01 us (3%)
    pallas_call x1, Pallas kernels, per_device(): pl.pallas_call(kernel, out_shape=(out, out, out, jax.ShapeDtypeStruct((HE...  133 us
    unnamed x4, local copies, waits for them, and re-layouts  4.01 us

profile of v4, /device:TPU:0, one launch (start us, length us, event | category | flops | bytes accessed | tf_op | source)
XLA Modules:
  0.0 137.2 jit_solution(12135585075429972253)
XLA Ops:
  0.6 132.6 %shard_map.111 = (bf16[256,3072]{1,0:T(8,128)(2,1)S(1)}, bf16[256,3072]{1,0:T(8,128)(2,1)S(1)}, bf16[256,3072]{1,0:T(8,128)(2,1)S(1)}, f32[3,128]{1,0:T(4,128)S(1)}) custom-call(bf16[256,3072]{1,0:T(8,128)(2,1)} %bitcast.11, bf16[256,3072]{1,0:T(8,128)(2,1)} %bitcast.12, bf16[256,3072]{1,0:T(8,128)(2,1)} %bitcast.13, bf16[256,3072]{1,0:T(8,128)(2,1)} %bitcast.14, ...), custom_call_target="tpu_custom_call" | custom-call | flops 7046430720 | bytes 11000000 | tf_op jit(solution)/shard_map/pallas_call | solution.py:501
  133.2 1.1 copy.16
  134.3 1.1 copy.17
  135.5 1.1 copy.18
  136.6 0.6 copy.19

commit v5 on v4

--- a/solution.py
+++ b/solution.py
@@ -35,7 +35,13 @@
 FROM_BELOW = tuple((q, s, q + o + SIDE) for q in range(SIDE) for s, o in enumerate(NEAR_OFFSETS) if q + o < 0)
 FROM_ABOVE = tuple((q, s, q + o - SIDE) for q in range(SIDE) for s, o in enumerate(NEAR_OFFSETS) if q + o >= SIDE)
 FROM_HALF = tuple((q, SLOTS - 1, q) for q in range(SIDE))
+FIRST = (0, 3, 6, 10)
 GROUPS = ((FROM_BELOW, 1), (FROM_ABOVE, SIDE - 1), (FROM_HALF, SIDE // 2))
+NEAR = tuple(
+    (q, s, tile, 1 + sum(tile == other[2] for other in group[:n]))
+    for group in (FROM_BELOW, FROM_ABOVE[::-1])
+    for n, (q, s, tile) in enumerate(group)
+)
 LOCAL = tuple(
     (q, s, q + o) for q in range(SIDE) for s, o in enumerate(NEAR_OFFSETS) if 0 <= q + o < SIDE
 )
@@ -48,16 +54,15 @@
 def kernel(
     queries, keys, values, upstream, table_hbm, slots_hbm, live_hbm, buckets_hbm,
     query_out, key_out, value_out, table_out,
-    kv_in, qd_in, give0, give1, give2, got0, got1, got2, back0, back1, back2, home0, home1, home2,
+    kv_in, qd_in, give0, give1, give2, got, back, home,
     ret, acc, key_set, value_set, key_part, value_part,
     table, slots, live, buckets, own_heads, own_far,
     tables, entries, shifted, fine, fine_sum, coarse_sum, grads, grads_dp, grads_seq,
     small_recv, own_recv,
-    kv_send, kv_recv, qd_send, qd_recv, give_send, got_recv, back_send, home_recv, far_recv, ret_send, out_recv,
+    kv_send, kv_recv, qd_send, qd_recv, give_send, got_recv, back_send, home_recv, ret_send, out_recv,
     table_send, table_recv, entry_send, entry_recv, dp_send, dp_recv, seq_send, seq_recv,
 ):
-    gives, gots = (give0, give1, give2), (got0, got1, got2)
-    backs, homes = (back0, back1, back2), (home0, home1, home2)
+    gives = (give0, give1, give2)
     outs = (query_out, key_out, value_out)
     place = lax.axis_index("seq")
     part = lax.axis_index("dp")
@@ -74,6 +79,8 @@
 
     def arrived(buffer, semaphore):
         pltpu.make_async_copy(buffer, buffer, semaphore).wait()
+
+    peers = slice(0, SIDE - 1)
 
     def head_columns(head):
         return pl.ds(pl.multiple_of(head * HEAD_DIM, HEAD_DIM), HEAD_DIM)
@@ -139,63 +146,73 @@
 
     def entry_copy(j):
         return remote(
-            entries.at[x], entries.at[x], entry_send.at[j], entry_recv.at[x], seq_at(x + j, y)
-        )
-
-    def fetch(refs, buffer, send, recv, c):
+            entries.at[x], entries.at[x], entry_send, entry_recv, seq_at(x + j, y)
+        )
+
+    def fetch(refs, buffer, send, recvs, c):
         for a, ref in enumerate(refs):
+            recv = recvs(c, a)
             for j in ORDER[:-1]:
                 to = lax.rem(x + j, SIDE)
                 remote(
                     ref.at[:, head_columns(to * CHUNKS + c)], buffer.at[c, a, x],
-                    send, recv.at[c, a], seq_at(to, y),
+                    send, recv, seq_at(to, y),
                 ).start()
             pltpu.make_async_copy(
-                ref.at[:, head_columns(x * CHUNKS + c)], buffer.at[c, a, x], recv.at[c, a]
+                ref.at[:, head_columns(x * CHUNKS + c)], buffer.at[c, a, x], recv
             ).start()
 
-    kv = ((keys, values), kv_in, kv_send, kv_recv)
-    qd = ((queries, upstream), qd_in, qd_send, qd_recv)
+    kv = ((keys, values), kv_in, kv_send, lambda c, a: kv_recv.at[c, a])
+    qd = ((queries, upstream), qd_in, qd_send, lambda c, a: qd_recv.at[c])
 
     def give_copy(g, c, a):
         return remote(
-            gives[g].at[c, a], gots[g].at[c, a], give_send.at[g], got_recv.at[c, g, a],
+            gives[g].at[c, a], got.at[c, a, FIRST[g] : FIRST[g + 1]], give_send.at[g],
+            got_recv.at[c],
             seq_at(x, y + GROUPS[g][1]),
         )
 
-    def back_copy(g, c, a):
+    def back_copy(c, tile, a, n):
+        row = SIDE // 2 if n == 0 else jnp.where(tile < 2, 1, SIDE - 1)
         return remote(
-            backs[g].at[c, a], homes[g].at[c, a], back_send.at[g], home_recv.at[c, g, a],
-            seq_at(x, y + SIDE - GROUPS[g][1]),
-        )
-
-    def far_back(c, a, tile):
-        return remote(
-            backs[2].at[c, a, tile], homes[2].at[c, a, tile], back_send.at[2],
-            far_recv.at[c, a, tile], seq_at(x, y + SIDE // 2),
-        )
+            back.at[c, tile, a, n], home.at[c, tile, a, n], back_send, home_recv.at[c, tile],
+            seq_at(x, y + row),
+        )
+
+    def outer(tile):
+        return (tile == 0) | (tile == SIDE - 1)
+
+    def near_pick(tile, n):
+        listing_row = y + jnp.where(tile < 2, SIDE - 1, 1)
+        if n == 1:
+            q = jnp.where(tile < 2, SIDE - 1, 0)
+            s = jnp.where(tile == 0, 1, jnp.where(tile == 1, 3, jnp.where(tile == 2, 2, 0)))
+        else:
+            q = jnp.where(tile == 0, 2, 1)
+            s = jnp.where(tile == 0, 3, 2)
+        return upper(listing_row, q, s)
 
     def give_back(a, c, j):
         columns = head_columns(x * CHUNKS + c)
         source = ret.at[c, a, lax.rem(x + j, SIDE)]
         if j == 0:
-            pltpu.make_async_copy(source, outs[a].at[:, columns], out_recv.at[a]).start()
+            outs[a][:, columns] = ret[c, a, x]
         else:
             remote(
                 source, outs[a].at[:, columns], ret_send.at[a], out_recv.at[a], seq_at(x + j, y)
             ).start()
 
-    table_copy(0).start()
-    for j in range(1, SIDE):
-        entry_copy(j).start()
     for c in range(CHUNKS):
         for a in range(2):
             remote(
-                own_far.at[a, c], gots[2].at[c, a, x], give_send.at[2], got_recv.at[c, 2, a],
+                own_far.at[a, c], got.at[c, a, FIRST[2] + x], give_send.at[2], got_recv.at[c],
                 seq_at(x, y + SIDE // 2),
             ).start()
         if c == 0:
             fetch(*kv, 0)
+    table_copy(0).start()
+    for j in range(1, SIDE):
+        entry_copy(j).start()
     fetch(*kv, 1)
     fetch(*kv, 2)
     fetch(*qd, 0)
@@ -220,8 +237,8 @@
                 pick = upper(y + SIDE // 2, tile, SLOTS - 1)
                 gives[2][c, a, tile] = jnp.where(pick, high, low)
                 remote(
-                    gives[2].at[c, a, tile], gots[2].at[c, a, tile], give_send.at[2],
-                    got_recv.at[c, 2, a], seq_at(x, y + SIDE // 2),
+                    gives[2].at[c, a, tile], got.at[c, a, FIRST[2] + tile], give_send.at[2],
+                    got_recv.at[c], seq_at(x, y + SIDE // 2),
                 ).start()
 
         @pl.when(c + 3 < CHUNKS)
@@ -233,10 +250,8 @@
             fetch(*qd, c + 1)
 
     def compute(c):
-        for a in range(2):
-            arrived(qd_in.at[c, a], qd_recv.at[c, a])
-            for g in range(3):
-                arrived(gots[g].at[c, a], got_recv.at[c, g, a])
+        arrived(qd_in.at[c], qd_recv.at[c])
+        arrived(got.at[c], got_recv.at[c])
         sets = (key_set, value_set)
         for a in range(2):
             for q in range(SIDE):
@@ -248,7 +263,7 @@
             for g, (group, _) in enumerate(GROUPS):
                 for n, (q, s, _) in enumerate(group):
                     at = (TILES_DEV + s) * TILE
-                    sets[a][q, at : at + TILE, :] = gots[g][c, a, n]
+                    sets[a][q, at : at + TILE, :] = got[c, a, FIRST[g] + n]
 
         head_row = tables[2 * x + lax.div(c, 3), pl.ds(lax.rem(c, 3), 1), :]
         for j in range(TILE_COLS):
@@ -329,22 +344,25 @@
             give_back(0, c, j)
         parts = (key_part, value_part)
 
-        def return_far(c, a, j):
+        def part_of(a, q, s):
+            at = (TILES_DEV + s) * TILE
+            return parts[a][q, at : at + TILE, :].astype(jnp.bfloat16)
+
+        for a in range(2):
+            for q, s, tile, n in NEAR:
+                back[c, tile, a, n] = part_of(a, q, s)
+            for q in range(SIDE):
+                back[c, q, a, 0] = part_of(a, q, SLOTS - 1)
+        for j in ORDER:
             tile = lax.rem(x + j, SIDE)
-            at = (ENTRIES - 1) * TILE
-            backs[2][c, a, tile] = parts[a][tile, at : at + TILE, :].astype(jnp.bfloat16)
-            far_back(c, a, tile).start()
-
-        for a in range(2):
-            for g, (group, _) in enumerate(GROUPS[:2]):
-                for n, (q, s, _) in enumerate(group):
-                    at = (TILES_DEV + s) * TILE
-                    backs[g][c, a, n] = parts[a][q, at : at + TILE, :].astype(jnp.bfloat16)
-                back_copy(g, c, a).start()
-            for j in ORDER[:-1]:
-                return_far(c, a, j)
-        for a in range(2):
-            return_far(c, a, 0)
+            for a in range(2):
+                back_copy(c, tile, a, 1).start()
+
+                @pl.when(outer(tile))
+                def _(a=a, tile=tile):
+                    back_copy(c, tile, a, 2).start()
+
+                back_copy(c, tile, a, 0).start()
         slot = lax.rem(c, 2)
         for a in range(2):
             for q in range(SIDE):
@@ -376,41 +394,40 @@
         acc[slot, a, tile, 0:TILE, :] += jnp.where(pick, 0.0, partial)
         acc[slot, a, tile, TILE : 2 * TILE, :] += jnp.where(pick, partial, 0.0)
 
-    def finish_tile(c, a, j):
-        slot = lax.rem(c, 2)
-        tile = lax.rem(x + j, SIDE)
-        arrived(homes[2].at[c, a, tile], far_recv.at[c, a, tile])
-        deposit(
-            slot, a, tile, upper(y + SIDE // 2, tile, SLOTS - 1),
-            homes[2][c, a, tile].astype(jnp.float32),
-        )
-        ret[c, 1 + a, tile] = acc[slot, a, tile].astype(jnp.bfloat16)
-        give_back(1 + a, c, j)
-
     def finish(c):
         slot = lax.rem(c, 2)
-        for a in range(2):
-            for g, (group, distance) in enumerate(GROUPS[:2]):
-                arrived(homes[g].at[c, a], home_recv.at[c, g, a])
-                for n, (q, s, tile) in enumerate(group):
+        for j in ORDER:
+            tile = lax.rem(x + j, SIDE)
+
+            @pl.when(outer(tile))
+            def _(tile=tile):
+                arrived(home.at[c, tile], home_recv.at[c, tile])
+                for a in range(2):
                     deposit(
-                        slot, a, tile, upper(y + distance, q, s),
-                        homes[g][c, a, n].astype(jnp.float32),
+                        slot, a, tile, near_pick(tile, 2),
+                        home[c, tile, a, 2].astype(jnp.float32),
                     )
-            for j in ORDER[:-1]:
-                finish_tile(c, a, j)
-        for a in range(2):
-            finish_tile(c, a, 0)
+
+            @pl.when(jnp.logical_not(outer(tile)))
+            def _(tile=tile):
+                arrived(home.at[c, tile, :, 0:2], home_recv.at[c, tile])
+
+            picks = (upper(y + SIDE // 2, tile, SLOTS - 1), near_pick(tile, 1))
+            for a in range(2):
+                for n, pick in enumerate(picks):
+                    deposit(slot, a, tile, pick, home[c, tile, a, n].astype(jnp.float32))
+                ret[c, 1 + a, tile] = acc[slot, a, tile].astype(jnp.bfloat16)
+                give_back(1 + a, c, j)
 
     def dp_copy(j):
         return remote(
-            grads, grads_dp.at[part], dp_send.at[j], dp_recv.at[part],
+            grads, grads_dp.at[part], dp_send, dp_recv,
             {"dp": lax.rem(part + j, DP)},
         )
 
     def seq_copy(j):
         return remote(
-            grads_seq.at[place], grads_seq.at[place], seq_send.at[j], seq_recv.at[place],
+            grads_seq.at[place], grads_seq.at[place], seq_send, seq_recv,
             {"seq": lax.rem(place + j, SEQ)},
         )
 
@@ -423,9 +440,7 @@
         def _():
             table_arrived(1)
             table_copy(2).start()
-            for j in range(1, SIDE):
-                source = lax.rem(x + j, SIDE)
-                arrived(entries.at[source], entry_recv.at[source])
+            arrived(entries.at[peers], entry_recv)
 
         @pl.when(t == 2)
         def _():
@@ -449,17 +464,14 @@
     lax.fori_loop(0, CHUNKS + 2, step, 0)
 
     total = grads[...]
+    arrived(grads_dp.at[0 : DP - 1], dp_recv)
     for j in range(1, DP):
-        source = lax.rem(part + j, DP)
-        arrived(grads_dp.at[source], dp_recv.at[source])
-        total = total + grads_dp[source]
+        total = total + grads_dp[lax.rem(part + j, DP)]
     grads_seq[place] = total
     for j in range(1, SEQ):
         seq_copy(j).start()
     finish(CHUNKS - 1)
-    for j in range(1, SEQ):
-        source = lax.rem(place + j, SEQ)
-        arrived(grads_seq.at[source], seq_recv.at[source])
+    arrived(grads_seq.at[0 : SEQ - 1], seq_recv)
     owner = lax.div(part, 2)
     mine = grads_seq[owner]
     for j in range(1, SIDE):
@@ -467,24 +479,20 @@
     own = HEADS // DP
     table_out[...] = jnp.where(lax.rem(part, 2) == 0, mine[0:own, :], mine[own : 2 * own, :])
 
-    peers = slice(0, SIDE - 1)
     arrived(kv_in.at[:, :, peers], kv_send)
     arrived(qd_in.at[:, :, peers], qd_send)
     for g in range(3):
         arrived(gives[g], give_send.at[g])
-        arrived(backs[g], back_send.at[g])
+    arrived(got, back_send)
     for a in range(3):
         arrived(ret.at[:, a, peers], ret_send.at[a])
     for n in range(len(STRIDES)):
         table_copy(n).wait_send()
-    for j in range(1, DP):
-        dp_copy(j).wait_send()
-    for j in range(1, SIDE):
-        entry_copy(j).wait_send()
-    for j in range(1, SEQ):
-        seq_copy(j).wait_send()
+    arrived(grads_dp.at[0 : DP - 1], dp_send)
+    arrived(entries.at[peers], entry_send)
+    arrived(grads_seq.at[0 : SEQ - 1], seq_send)
     for a in range(3):
-        arrived(outs[a], out_recv.at[a])
+        arrived(outs[a].at[0 : TOK_DEV - TOK_DEV // SIDE], out_recv.at[a])
 
 
 def per_device(queries, keys, values, grad_out, bias_table, slot_tiles, live, buckets):
@@ -506,7 +514,10 @@
         scratch_shapes=[
             pltpu.VMEM((CHUNKS, 2, SIDE, TOK_DEV, HEAD_DIM), low),
             pltpu.VMEM((CHUNKS, 2, SIDE, TOK_DEV, HEAD_DIM), low),
-            *moved, *moved, *moved, *moved,
+            *moved,
+            pltpu.VMEM((CHUNKS, 2, FIRST[-1], TILE, HEAD_DIM), low),
+            pltpu.VMEM((CHUNKS, SIDE, 2, 3, TILE, HEAD_DIM), low),
+            pltpu.VMEM((CHUNKS, SIDE, 2, 3, TILE, HEAD_DIM), low),
             pltpu.VMEM((CHUNKS, 3, SIDE, TOK_DEV, HEAD_DIM), low),
             pltpu.VMEM((2, 2, SIDE, TOK_DEV, HEAD_DIM), full),
             pltpu.VMEM((SIDE, set_rows, HEAD_DIM), low),
@@ -530,14 +541,14 @@
             pltpu.VMEM((SEQ, 8, TABLE), full),
             dma((4,)), dma(()),
             dma(()), dma((CHUNKS, 2)),
-            dma(()), dma((CHUNKS, 2)),
-            dma((3,)), dma((CHUNKS, 3, 2)),
-            dma((3,)), dma((CHUNKS, 2, 2)), dma((CHUNKS, 2, SIDE)),
+            dma(()), dma((CHUNKS,)),
+            dma((3,)), dma((CHUNKS,)),
+            dma(()), dma((CHUNKS, SIDE)),
             dma((3,)), dma((3,)),
             dma((len(STRIDES),)), dma((len(STRIDES),)),
-            dma((SIDE,)), dma((SIDE,)),
-            dma((DP,)), dma((DP,)),
-            dma((SEQ,)), dma((SEQ,)),
+            dma(()), dma(()),
+            dma(()), dma(()),
+            dma(()), dma(()),
         ],
         compiler_params=pltpu.CompilerParams(
             collective_id=0, has_side_effects=True, vmem_limit_bytes=48 * 2**20

time: 137 us -> 137 us (level)
  no operation moved by 1% of the time
where the time goes in v5:
time: 137 us; the launch traced here: 136 us
  Pallas kernels  132 us (96%)
  local copies, waits for them, and re-layouts  4.01 us (3%)
    pallas_call x1, Pallas kernels, per_device(): pl.pallas_call(kernel, out_shape=(out, out, out, jax.ShapeDtypeStruct((HE...  132 us
    unnamed x4, local copies, waits for them, and re-layouts  4.01 us

profile of v5, /device:TPU:0, one launch (start us, length us, event | category | flops | bytes accessed | tf_op | source)
XLA Modules:
  0.0 136.3 jit_solution(3921583609787925355)
XLA Ops:
  0.6 131.7 %shard_map.111 = (bf16[256,3072]{1,0:T(8,128)(2,1)S(1)}, bf16[256,3072]{1,0:T(8,128)(2,1)S(1)}, bf16[256,3072]{1,0:T(8,128)(2,1)S(1)}, f32[3,128]{1,0:T(4,128)S(1)}) custom-call(bf16[256,3072]{1,0:T(8,128)(2,1)} %bitcast.11, bf16[256,3072]{1,0:T(8,128)(2,1)} %bitcast.12, bf16[256,3072]{1,0:T(8,128)(2,1)} %bitcast.13, bf16[256,3072]{1,0:T(8,128)(2,1)} %bitcast.14, ...), custom_call_target="tpu_custom_call" | custom-call | flops 7046430720 | bytes 11000000 | tf_op jit(solution)/shard_map/pallas_call | solution.py:509
  132.3 1.1 copy.16
  133.4 1.1 copy.17
  134.6 1.1 copy.18
  135.7 0.6 copy.19

commit v6 on v5

--- a/solution.py
+++ b/solution.py
@@ -356,9 +356,13 @@
         for j in ORDER:
             tile = lax.rem(x + j, SIDE)
             for a in range(2):
-                back_copy(c, tile, a, 1).start()
-
-                @pl.when(outer(tile))
+                lists = jnp.where(tile < 2, y != SIDE - 1, y != 0)
+
+                @pl.when(lists)
+                def _(a=a, tile=tile):
+                    back_copy(c, tile, a, 1).start()
+
+                @pl.when(lists & outer(tile))
                 def _(a=a, tile=tile):
                     back_copy(c, tile, a, 2).start()
 
@@ -399,23 +403,31 @@
         for j in ORDER:
             tile = lax.rem(x + j, SIDE)
 
-            @pl.when(outer(tile))
+            listed = jnp.where(tile < 2, y != 0, y != SIDE - 1)
+
+            def near(n, tile=tile):
+                pick = near_pick(tile, n)
+                for a in range(2):
+                    deposit(slot, a, tile, pick, home[c, tile, a, n].astype(jnp.float32))
+
+            @pl.when(listed & outer(tile))
+            def _(tile=tile, near=near):
+                arrived(home.at[c, tile], home_recv.at[c, tile])
+                near(1)
+                near(2)
+
+            @pl.when(listed & jnp.logical_not(outer(tile)))
+            def _(tile=tile, near=near):
+                arrived(home.at[c, tile, :, 0:2], home_recv.at[c, tile])
+                near(1)
+
+            @pl.when(jnp.logical_not(listed))
             def _(tile=tile):
-                arrived(home.at[c, tile], home_recv.at[c, tile])
-                for a in range(2):
-                    deposit(
-                        slot, a, tile, near_pick(tile, 2),
-                        home[c, tile, a, 2].astype(jnp.float32),
-                    )
-
-            @pl.when(jnp.logical_not(outer(tile)))
-            def _(tile=tile):
-                arrived(home.at[c, tile, :, 0:2], home_recv.at[c, tile])
-
-            picks = (upper(y + SIDE // 2, tile, SLOTS - 1), near_pick(tile, 1))
+                arrived(home.at[c, tile, :, 0:1], home_recv.at[c, tile])
+
+            far_pick = upper(y + SIDE // 2, tile, SLOTS - 1)
             for a in range(2):
-                for n, pick in enumerate(picks):
-                    deposit(slot, a, tile, pick, home[c, tile, a, n].astype(jnp.float32))
+                deposit(slot, a, tile, far_pick, home[c, tile, a, 0].astype(jnp.float32))
                 ret[c, 1 + a, tile] = acc[slot, a, tile].astype(jnp.bfloat16)
                 give_back(1 + a, c, j)
 
@@ -483,7 +495,16 @@
     arrived(qd_in.at[:, :, peers], qd_send)
     for g in range(3):
         arrived(gives[g], give_send.at[g])
-    arrived(got, back_send)
+    ends = (y == 0) | (y == SIDE - 1)
+
+    @pl.when(ends)
+    def _():
+        arrived(got.at[:, :, FIRST[1] :], back_send)
+
+    @pl.when(jnp.logical_not(ends))
+    def _():
+        arrived(got, back_send)
+
     for a in range(3):
         arrived(ret.at[:, a, peers], ret_send.at[a])
     for n in range(len(STRIDES)):

time: 137 us -> 136 us (level)
  no operation moved by 1% of the time
where the time goes in v6:
time: 136 us
  Pallas kernels  131 us (96%)
  local copies, waits for them, and re-layouts  4.01 us (3%)
    pallas_call x1, Pallas kernels, per_device(): pl.pallas_call(kernel, out_shape=(out, out, out, jax.ShapeDtypeStruct((HE...  131 us
    unnamed x4, local copies, waits for them, and re-layouts  4.01 us

profile of v6, /device:TPU:0, one launch (start us, length us, event | category | flops | bytes accessed | tf_op | source)
XLA Modules:
  0.0 135.7 jit_solution(17821332378162662582)
XLA Ops:
  0.6 131.0 %shard_map.111 = (bf16[256,3072]{1,0:T(8,128)(2,1)S(1)}, bf16[256,3072]{1,0:T(8,128)(2,1)S(1)}, bf16[256,3072]{1,0:T(8,128)(2,1)S(1)}, f32[3,128]{1,0:T(4,128)S(1)}) custom-call(bf16[256,3072]{1,0:T(8,128)(2,1)} %bitcast.11, bf16[256,3072]{1,0:T(8,128)(2,1)} %bitcast.12, bf16[256,3072]{1,0:T(8,128)(2,1)} %bitcast.13, bf16[256,3072]{1,0:T(8,128)(2,1)} %bitcast.14, ...), custom_call_target="tpu_custom_call" | custom-call | flops 7046430720 | bytes 11000000 | tf_op jit(solution)/shard_map/pallas_call | solution.py:530
  131.7 1.1 copy.16
  132.8 1.1 copy.17
  134.0 1.1 copy.18
  135.1 0.6 copy.19
